TPU v7x, 512 devices: a whole 4x4x16 slice. The times are simulated.
512 devices in a mesh: prow: 32 (over z, core), pcol: 16 (over x, y).
Axes of the slice: x: 4, y: 4, z: 16, core: 2. Of those that a mesh axis runs over, the one named last changes fastest.
Arguments:
- trailing: bfloat16 [8, 8192, 2, 4096], P(None, 'prow', None, 'pcol'), may hold values from -6 to 6
- panel: bfloat16 [256, 8, 8192], P('pcol', None, 'prow'), may hold values from -1 to 1
- lower_inverse: bfloat16 [256, 256], replicated
- upper_inverse: bfloat16 [256, 256], replicated
- pivots: int32 [256], replicated, may hold values from 0 to 65535, as said below
Outputs:
- updated: bfloat16 [8, 8192, 2, 4096], P(None, 'prow', None, 'pcol')
Inputs may be any that keep to these rules, and one draw needn't show every extreme that they name: `pivots`: the entries are distinct; entry i is either i or a row index of 256 or more. Entry 0 is 0 and entry 1 is 65535.
All inputs are finite; a program needn't handle non-finite values.
Results may differ from a plain program's by a relative error of at most 0.0054.
Values may be sent and summed in bfloat16 or wider, within the bound.
A program may use at most 64 MiB of HBM per device.

v0:
```python
import jax
import jax.numpy as jnp
from jax import lax
from jax.sharding import PartitionSpec as P


def from_root(x, axis, root):
    mine = lax.axis_index(axis) == root
    return lax.psum(jnp.where(mine, x, jnp.zeros_like(x)), axis)


def contract_lead(left_side, right_side):
    return lax.dot_general(
        left_side, right_side, (((0,), (0,)), ((), ())), preferred_element_type=jnp.float32
    )


def per_device(trailing, panel, lower_inverse, upper_inverse, pivots):
    row_blocks, block_size, col_blocks, col_size = trailing.shape
    local_rows = row_blocks * block_size
    matrix = trailing.reshape(local_rows, col_blocks * col_size)
    panel_rows = panel.reshape(panel.shape[0], local_rows)
    prow_count = lax.axis_size("prow")
    prow_index = lax.axis_index("prow")
    head_rows = jnp.arange(block_size, dtype=jnp.int32)
    pivot_owner = pivots // block_size % prow_count
    pivot_local = pivots // (block_size * prow_count) * block_size + pivots % block_size
    pivot_here = pivot_owner == prow_index
    fetched = jnp.take(matrix, jnp.where(pivot_here, pivot_local, 0), axis=0)
    picked = jnp.where(pivot_here[:, None], fetched, jnp.zeros_like(fetched))
    old_top = matrix[:block_size]
    at_root = prow_index == 0
    source = picked[None]
    gathered_top = lax.psum(source, "prow").astype(jnp.float32).astype(jnp.bfloat16)
    solved = jnp.dot(lower_inverse, gathered_top[0], preferred_element_type=jnp.float32).astype(
        jnp.bfloat16
    )
    root_top = from_root(old_top, "prow", 0)
    local_index = jnp.arange(local_rows, dtype=jnp.int32)
    global_rows = (
        local_index // block_size * prow_count + prow_index
    ) * block_size + local_index % block_size
    matches = (global_rows[:, None] == pivots[None, :]) & (pivots != head_rows)[None, :]
    incoming = jnp.sum(jnp.where(matches, head_rows[None, :], 0), axis=1)
    has_incoming = jnp.any(matches, axis=1)
    swapped = jnp.where(has_incoming[:, None], jnp.take(root_top, incoming, axis=0), matrix)
    lower_t = contract_lead(upper_inverse, lax.all_gather(panel_rows, "pcol", axis=0, tiled=True))
    lower_t = lower_t.astype(jnp.bfloat16)
    product = contract_lead(lower_t, solved)
    updated = (swapped.astype(jnp.float32) - product).astype(jnp.bfloat16)
    top_block = jnp.where(at_root, solved, updated[:block_size])
    updated = lax.dynamic_update_slice_in_dim(updated, top_block, 0, 0)
    return updated.reshape(trailing.shape)


def solution(mesh):
    placed = (P(None, "prow", None, "pcol"), P("pcol", None, "prow"), P(), P(), P())
    return jax.shard_map(
        per_device,
        mesh=mesh,
        in_specs=placed,
        out_specs=P(None, "prow", None, "pcol"),
        check_vma=False,
    )
```

profile of v0, /device:TPU:1, one launch (start us, length us, event | category | flops | bytes accessed | tf_op | source)
XLA Modules:
  0.0 261.1 jit_solution(12199682226288083791)
XLA Ops:
  7.4 0.7 compare_and_fusion.2
  8.1 1.2 broadcast_select_fusion
  9.3 0.7 copy.23
  10.0 2.0 copy.24
  12.1 1.2 gather_fusion.1
  13.2 0.8 fusion.3
  14.1 0.0 all-reduce.3.cloned.1.call-update
  14.1 0.0 all-gather.2.cloned.1.call-start
  14.2 0.6 copy.25
  14.8 0.0 all-gather.2.cloned.1.call-update
  14.8 0.0 copy-start.5
  14.8 2.4 copy.22
  17.2 0.8 fusion
  18.0 0.9 select_reduce_fusion
  18.9 212.9 %all-reduce.3.cloned.1.call-done = (bf16[256,512]{1,0:T(8,128)(2,1)}, bf16[256,512]{1,0:T(8,128)(2,1)}) async-done(((bf16[256,512]{1,0:T(8,128)(2,1)}, bf16[256,512]{1,0:T(8,128)(2,1)}), (bf16[256,512]{1,0:T(8,128)(2,1)}, bf16[256,512]{1,0:T(8,128)(2,1)})) %all-reduce.3.cloned.1.call-update) | async-done | bytes 524304 | tf_op jit(solution)/shard_map/psum | solution.py:34
  231.8 8.6 %gather_fusion = bf16[2048,512]{1,0:T(8,128)(2,1)S(1)} fusion(bf16[256,512]{1,0:T(8,128)(2,1)} %get-tuple-element.6, s32[2048]{0:T(1024)S(1)} %broadcast_clamp_fusion), kind=kCustom, calls=%fused_computation | custom fusion | bytes 4202496 | tf_op jit(solution)/shard_map/jit(_take)/gather | solution.py:46
  240.4 2.5 copy.16
  242.8 0.3 convolution_convert_fusion.1
  243.1 0.0 all-gather.2.cloned.1.call-done
  243.2 3.8 %subtract_convert_fusion = bf16[2048,512]{0,1:T(8,128)(2,1)S(1)} fusion(bf16[512,256]{1,0:T(8,128)(2,1)S(1)} %convolution_convert_fusion.1, bf16[2048,512]{0,1:T(8,128)(2,1)} %copy.22, bf16[2048,512]{0,1:T(8,128)(2,1)} %copy.16, pred[2048]{0:T(1024)(128)(4,1)S(1)} %compare_and_fusion.1, pred[2048]{0:T(1024)(128)(4,1)S(1)} %fusion, ...), kind=kOutput, calls=%fused_computation.2 | convolution fusion | flops 811073536 | bytes 7737344 | tf_op jit(solution)/shard_map/dot_general | solution.py:13
  246.9 0.1 fusion.1
  247.1 1.3 copy-done.1
  248.4 2.3 copy.26
  250.7 3.0 %copy.20 = bf16[8,256,2,256]{3,2,1,0:T(2,128)(2,1)} copy(bf16[8,256,2,256]{1,0,3,2:T(8,128)(2,1)S(1)} %bitcast.32) | data formatting | bytes 4194304 | tf_op jit(solution)/shard_map/reshape | solution.py:53
  (16 shorter events, 0.1 us)
Async XLA Ops:
  7.4 235.8 %copy-start = (bf16[256,256]{1,0:T(8,128)(2,1)S(1)}, bf16[256,256]{1,0:T(8,128)(2,1)}, u32[]{:S(2)}) copy-start(bf16[256,256]{1,0:T(8,128)(2,1)} %param.8) | copy-start | bytes 393220
  7.4 224.4 %all-reduce.3.cloned.1.call-start = ((), (), s32[]{:S(2)}) async-start(), calls=%async_computation.1 | async-start | bytes 1048576 | tf_op jit(solution)/shard_map/psum | solution.py:34
  12.1 2.1 copy-start.4
  14.1 229.0 %all-gather.2.cloned.1.call-start = ((), (), s32[]{:S(2)}) async-start(), calls=%async_computation | async-start | bytes 1114112 | tf_op jit(solution)/shard_map/all_gather | solution.py:47
  14.8 2.4 copy-start.5
  240.4 2.5 copy-start.2
  240.4 2.5 copy-start.3
  247.1 1.3 copy-start.1
Sparse Core Ops, SparseCore 0:
  14.2 217.5 all-reduce.2
Sparse Core Ops, SparseCore 1:
  17.6 61.1 all-gather.1
where the time goes:
time: 261 us
  waiting for transfers between devices  213 us (82%)
  local copies, waits for them, and re-layouts  24.5 us (9%)
  between operations  15 us (6%)
  other arithmetic  4.52 us (2%)
  matrix products  4.05 us (2%)
    psum x1, waiting for transfers between devices, per_device(): lax.psum(source, 'prow').astype(jnp.float32).astype(jnp.bfloat16)  213 us
    gather x2, local copies, waits for them, and re-layouts, per_device(): jnp.take(root_top, incoming, axis=0)  11 us
    unnamed x16, local copies, waits for them, and re-layouts  7.01 us
  transfers between devices with their start and end apart: 2, of which 1 were waited for; matrix products, arithmetic and copies ran while one was open for 6% of the time, Pallas kernels for 0%

commit v1 on v0

v1 whole, which is shorter than its diff:
```python
import functools

import jax
import jax.numpy as jnp
from jax import lax
from jax.experimental import pallas as pl
from jax.experimental.pallas import tpu as pltpu
from jax.sharding import PartitionSpec as P

NB = 256
CAP = 24
NZ, NX, NY = 16, 4, 4
NPROW = 2 * NZ
FAR = NZ // 2
SLOT = CAP * 4
TCH = 8
TROWS = 512 // TCH
GROUP = 4
BF, F32 = jnp.bfloat16, jnp.float32
VMEM, ANY, SMEM = pltpu.VMEM, pl.ANY, pltpu.SMEM


def spec(space):
    return pl.BlockSpec(memory_space=space)


def remote(src, dst, ss, rs, **where):
    return pltpu.make_async_remote_copy(
        src_ref=src, dst_ref=dst, send_sem=ss, recv_sem=rs,
        device_id=where, device_id_type=pl.DeviceIdType.MESH,
    )


def onehot(cond, value=1.0):
    return jnp.where(cond, value, 0.0).astype(BF)


def column_of(row):
    n = row.shape[1]
    eye = lax.broadcasted_iota(jnp.int32, (n, n), 0) == lax.broadcasted_iota(jnp.int32, (n, n), 1)
    return jnp.sum(jnp.where(eye, jnp.broadcast_to(row, (n, n)), 0), axis=1, keepdims=True)


def owner_of(piv):
    return (piv >> 8) & (NPROW - 1)


def ranks(row, col):
    i0 = lax.broadcasted_iota(jnp.int32, (NB, NB), 0)
    i1 = lax.broadcasted_iota(jnp.int32, (NB, NB), 1)
    before = (owner_of(col) == owner_of(row)) & (i1 < i0) & (row != i1)
    return jnp.dot(onehot(before), jnp.ones((NB, 128), BF), preferred_element_type=F32)


def pick_kernel(piv_ref, t_ref, row_ref, x_ref, o_ref, rounds_ref, idx_ref, sem):
    me = lax.axis_index("prow")
    first = t_ref[0] * CAP
    for s in range(CAP + 1):
        idx_ref[s] = 0

    def step(i, n):
        p = piv_ref[i]
        mine = (((p >> 8) & (NPROW - 1)) == me) & (p != i)
        at = n - first
        slot = jnp.where((at >= 0) & (at < CAP), at, CAP)
        idx_ref[slot] = ((p >> 13) << 8) + (p & 255)
        return n + jnp.where(mine, 1, 0)

    n = lax.fori_loop(0, NB, step, 0, unroll=8)

    @pl.when((n >= first) & (n < first + CAP))
    def _():
        idx_ref[n - first] = 0

    copies = []
    for s in range(CAP):
        r = idx_ref[s]
        copies.append(pltpu.make_async_copy(x_ref.at[r >> 8, r & 255], o_ref.at[s], sem.at[s]))
        copies[-1].start()
    row = row_ref[...]
    rank = ranks(row, column_of(row))
    rounds_ref[0] = jnp.max(rank).astype(jnp.int32) // CAP + 1
    for c in copies:
        c.wait()


def pick(trailing, pivots, t):
    out, rounds = pl.pallas_call(
        pick_kernel,
        out_shape=(
            jax.ShapeDtypeStruct((CAP, 2, 256), BF),
            jax.ShapeDtypeStruct((1,), jnp.int32),
        ),
        in_specs=[spec(SMEM), spec(SMEM), spec(VMEM), spec(ANY)],
        out_specs=(spec(VMEM), spec(SMEM)),
        scratch_shapes=[SMEM((CAP + 1,), jnp.int32), pltpu.SemaphoreType.DMA((CAP,))],
        compiler_params=pltpu.CompilerParams(vmem_limit_bytes=16 * 2**20),
        name="pick_rows",
    )(pivots, t, pivots.reshape(1, NB), trailing)
    return out.reshape(CAP, 2, 2, 128).transpose(0, 2, 1, 3).reshape(SLOT, 128), rounds


class Ring:
    def __init__(self, src, slots, zs, zr, ps, pr):
        self.src, self.slots, self.zs, self.zr, self.ps, self.pr = src, slots, zs, zr, ps, pr
        me = lax.axis_index("prow")
        self.z, self.core = me // 2, me % 2
        self.sent = []

    def rows(self, z, core):
        return self.slots.at[pl.ds(((z % NZ) * 2 + core) * SLOT, SLOT)]

    def hop(self, way, s, src=None):
        sign = 1 - 2 * way
        dst = self.rows(self.z + NZ - sign * s, self.core)
        to = ((self.z + NZ + sign) % NZ) * 2 + self.core
        c = remote(dst if src is None else src, dst, self.zs.at[way, s], self.zr.at[way, s], prow=to)
        c.start()
        self.sent.append(c)

    def mate(self, k, offset, src=None):
        dst = self.rows(self.z + NZ + offset, self.core)
        c = remote(
            dst if src is None else src, dst, self.ps.at[k], self.pr.at[k],
            prow=self.z * 2 + 1 - self.core,
        )
        c.start()
        self.sent.append(c)

    def begin(self):
        self.hop(0, 0, self.src)
        self.hop(1, 0, self.src)
        self.mate(0, 0, self.src)

    def arrive(self, way, s):
        sign = 1 - 2 * way
        dst = self.rows(self.z + NZ - sign * s, self.core)
        remote(
            dst, dst, self.zs.at[way, s - 1], self.zr.at[way, s - 1], prow=self.z * 2 + self.core
        ).wait_recv()

    def step(self, s):
        if s > FAR:
            return
        self.arrive(0, s)
        if s < FAR:
            self.hop(0, s)
        self.mate(s, -s)
        if s < FAR:
            self.arrive(1, s)
            if s < FAR - 1:
                self.hop(1, s)
            self.mate(FAR + s, s)

    def finish(self):
        for k in range(NZ):
            offset = -k if k <= FAR else k - FAR
            dst = self.rows(self.z + NZ + offset, 1 - self.core)
            remote(
                dst, dst, self.ps.at[k], self.pr.at[k], prow=self.z * 2 + self.core
            ).wait_recv()
        for c in self.sent:
            c.wait_send()


RING_SEMS = [
    pltpu.SemaphoreType.DMA((2, FAR)),
    pltpu.SemaphoreType.DMA((2, FAR)),
    pltpu.SemaphoreType.DMA((NZ,)),
    pltpu.SemaphoreType.DMA((NZ,)),
]


def greet(ids):
    barrier = pltpu.get_barrier_semaphore()
    for where in ids:
        pl.semaphore_signal(barrier, inc=1, device_id=where, device_id_type=pl.DeviceIdType.MESH)
    pl.semaphore_wait(barrier, len(ids))


def z_neighbours():
    me = lax.axis_index("prow")
    z, core = me // 2, me % 2
    return [
        {"prow": ((z + 1) % NZ) * 2 + core},
        {"prow": ((z + NZ - 1) % NZ) * 2 + core},
        {"prow": z * 2 + 1 - core},
    ]


def gather_kernel(src_ref, o_ref, slots, zs, zr, ps, pr, sem):
    greet(z_neighbours())
    ring = Ring(src_ref, slots, zs, zr, ps, pr)
    ring.begin()
    own = pltpu.make_async_copy(src_ref, ring.rows(ring.z, ring.core), sem)
    own.start()
    for s in range(1, FAR + 1):
        ring.step(s)
    own.wait()
    ring.finish()
    o_ref[...] = slots[...]


def gather_round(picked):
    return pl.pallas_call(
        gather_kernel,
        out_shape=jax.ShapeDtypeStruct((NPROW * SLOT, 128), BF),
        in_specs=[spec(VMEM)],
        out_specs=spec(VMEM),
        scratch_shapes=[VMEM((NPROW * SLOT, 128), BF)] + RING_SEMS + [pltpu.SemaphoreType.DMA],
        compiler_params=pltpu.CompilerParams(collective_id=1, has_side_effects=True),
        name="gather_more",
    )(picked)


def later_rounds(trailing, pivots, rounds):
    i = jnp.arange(NB, dtype=jnp.int32)
    owner = owner_of(pivots)
    moved = pivots != i
    before = (owner[:, None] == owner[None, :]) & (i[None, :] < i[:, None]) & moved[None, :]
    rank = jnp.sum(before.astype(jnp.int32), axis=1)

    def body(carry):
        t, total = carry
        picked, _ = pick(trailing, pivots, t.reshape(1))
        rows = gather_round(picked).reshape(NPROW * CAP, 512)
        at = rank - t * CAP
        slot = jnp.where(moved & (at >= 0) & (at < CAP), owner * CAP + at, -1)
        chosen = onehot(slot[:, None] == jnp.arange(NPROW * CAP, dtype=jnp.int32)[None, :])
        part = jnp.dot(chosen, rows, preferred_element_type=F32).astype(BF)
        return t + 1, total + part.reshape(NB * 4, 128)

    start = (jnp.int32(1), jnp.zeros((NB * 4, 128), BF))
    return lax.while_loop(lambda c: c[0] < rounds[0], body, start)[1]


class Plane:
    OFF = (0, -1, 1, 2)

    def __init__(self, src, out, ss, rs):
        self.src, self.out, self.ss, self.rs = src, out, ss, rs
        q = lax.axis_index("pcol")
        self.x, self.y = q // NY, q % NY
        self.sent = []

    def device(self, h, first, second):
        dx, dy = (second, first) if h == 0 else (first, second)
        return ((self.x + NX + dx) % NX) * NY + (self.y + NY + dy) % NY

    def part(self, h, first, second, quarter=None):
        base = self.device(h, first, second) * 256 + h * 128
        if quarter is None:
            return self.out.at[pl.ds(base, 128)]
        return self.out.at[pl.ds(base + 64 * quarter, 64)]

    def send(self, h, k, to, ref, src=None):
        c = remote(ref if src is None else src, ref, self.ss.at[h, k], self.rs.at[h, k], pcol=to)
        c.start()
        self.sent.append(c)

    def wait(self, h, k, ref):
        remote(ref, ref, self.ss.at[h, k], self.rs.at[h, k], pcol=self.device(h, 0, 0)).wait_recv()

    def second(self, h, m, src=None):
        ref = self.part(h, self.OFF[m], 0)
        self.send(h, 4 + m, self.device(h, 0, 1), ref, src)
        self.send(h, 8 + m, self.device(h, 0, -1), ref, src)

    def begin(self):
        for h in range(2):
            own = self.src.at[pl.ds(h * 128, 128)]
            self.send(h, 0, self.device(h, 1, 0), self.part(h, 0, 0), own)
            self.send(h, 1, self.device(h, -1, 0), self.part(h, 0, 0), own)
        for h in range(2):
            self.second(h, 0, self.src.at[pl.ds(h * 128, 128)])

    def one(self):
        for h in range(2):
            self.wait(h, 0, self.part(h, -1, 0))
            self.send(h, 2, self.device(h, 1, 0), self.part(h, -1, 0, 0))
            self.wait(h, 1, self.part(h, 1, 0))
            self.send(h, 3, self.device(h, -1, 0), self.part(h, 1, 0, 1))
        for h in range(2):
            self.second(h, 1)
            self.second(h, 2)

    def two(self):
        for h in range(2):
            self.wait(h, 2, self.part(h, -2, 0, 0))
            self.wait(h, 3, self.part(h, 2, 0, 1))
            self.second(h, 3)

    def three(self, m):
        for h in range(2):
            f = self.OFF[m]
            self.wait(h, 4 + m, self.part(h, f, -1))
            self.send(h, 12 + m, self.device(h, 0, 1), self.part(h, f, -1, 0))
            self.wait(h, 8 + m, self.part(h, f, 1))
            self.send(h, 16 + m, self.device(h, 0, -1), self.part(h, f, 1, 1))

    def four(self):
        for h in range(2):
            for m in range(4):
                self.wait(h, 12 + m, self.part(h, self.OFF[m], -2, 0))
                self.wait(h, 16 + m, self.part(h, self.OFF[m], 2, 1))

    def finish(self):
        for c in self.sent:
            c.wait_send()


def plane_neighbours():
    q = lax.axis_index("pcol")
    x, y = q // NY, q % NY
    return [
        {"pcol": ((x + 1) % NX) * NY + y},
        {"pcol": ((x + NX - 1) % NX) * NY + y},
        {"pcol": x * NY + (y + 1) % NY},
        {"pcol": x * NY + (y + NY - 1) % NY},
    ]


class Top:
    def __init__(self, src, out, ss, rr, ps, pr):
        self.src, self.out, self.ss, self.rr, self.ps, self.pr = src, out, ss, rr, ps, pr
        me = lax.axis_index("prow")
        self.z, self.core = me // 2, me % 2
        self.dist = jnp.where(self.z <= FAR, self.z, NZ - self.z)
        self.root = me == 0
        self.right = self.z < FAR
        self.left = (self.z == 0) | (self.z > FAR + 1)

    def rows(self, ref, half, n):
        return ref.at[pl.ds(half * 512 + n * TROWS, TROWS)]

    def ring(self, way, n, src):
        to = ((self.z + NZ + 1 - 2 * way) % NZ) * 2 + self.core
        return remote(
            self.rows(src, self.core, n), self.rows(self.out, self.core, n),
            self.ss.at[way, n], self.rr.at[n], prow=to,
        )

    def mate(self, half, n, src, rsem):
        return remote(
            self.rows(src, half, n), self.rows(self.out, half, n),
            self.ps.at[half, n], rsem.at[n], prow=self.z * 2 + 1 - self.core,
        )

    def begin(self):
        @pl.when(self.root)
        def _():
            for n in range(TCH):
                self.mate(1, n, self.src, self.rr).start()
                self.ring(0, n, self.src).start()
                self.ring(1, n, self.src).start()
            for n in range(TCH):
                self.mate(0, n, self.src, self.pr).start()

    def own(self, sem):
        return pltpu.make_async_copy(self.src.at[pl.ds(0, 1024)], self.out, sem)

    def step(self, s):
        for g in range(TCH // GROUP):
            @pl.when((self.dist + g == s) & ~self.root)
            def _():
                for n in range(g * GROUP, (g + 1) * GROUP):
                    self.ring(0, n, self.out).wait_recv()

                    @pl.when(self.right)
                    def _():
                        self.ring(0, n, self.out).start()

                    @pl.when(self.left)
                    def _():
                        self.ring(1, n, self.out).start()

                    @pl.when(self.z != 0)
                    def _():
                        self.mate(self.core, n, self.out, self.pr).start()

    def finish(self):
        @pl.when(~self.root)
        def _():
            for n in range(TCH):
                self.mate(1 - self.core, n, self.out, self.pr).wait_recv()

        @pl.when(self.right)
        def _():
            for n in range(TCH):
                self.ring(0, n, self.out).wait_send()

        @pl.when(self.left)
        def _():
            for n in range(TCH):
                self.ring(1, n, self.out).wait_send()

        @pl.when(self.z != 0)
        def _():
            for n in range(TCH):
                self.mate(self.core, n, self.out, self.pr).wait_send()

        @pl.when(self.root)
        def _():
            for n in range(TCH):
                self.mate(0, n, self.src, self.pr).wait_send()
                self.mate(1, n, self.src, self.rr).wait_send()


TOP_SEMS = [
    pltpu.SemaphoreType.DMA((2, TCH)),
    pltpu.SemaphoreType.DMA((TCH,)),
    pltpu.SemaphoreType.DMA((2, TCH)),
    pltpu.SemaphoreType.DMA((TCH,)),
]


def main_kernel(
    x_ref, pick_ref, panel_ref, linv_ref, uinv_ref, row_ref, extra_ref,
    m_ref, xm_ref, st_ref,
    slots, top, panel, panelf, wide, both, mask,
    zs, zr, zps, zpr, ts, tr, tps, tpr, ss, rs, sems,
):
    me = lax.axis_index("prow")
    fetch = pltpu.make_async_copy(x_ref, xm_ref, sems.at[0])
    fetch.start()
    greet(z_neighbours() + plane_neighbours())
    ring = Ring(pick_ref, slots, zs, zr, zps, zpr)
    plane = Plane(panel_ref, panel, ss, rs)
    head = Top(x_ref, top, ts, tr, tps, tpr)
    head.begin()
    ring.begin()
    plane.begin()
    q = lax.axis_index("pcol")
    own_panel = pltpu.make_async_copy(panel_ref, panel.at[pl.ds(q * 256, 256)], sems.at[1])
    own_panel.start()
    own_slot = pltpu.make_async_copy(pick_ref, ring.rows(ring.z, ring.core), sems.at[2])
    own_slot.start()

    @pl.when(head.root)
    def _():
        head.own(sems.at[3]).start()

    row = row_ref[...]
    lanes = lax.broadcasted_iota(jnp.int32, (1, NB), 1)
    moved = row != lanes

    def swaps(b):
        rows = lax.broadcasted_iota(jnp.int32, (NB, NB), 0) + (b * NPROW + me) * NB
        hit = (rows == row) & moved
        m_ref[pl.ds(b * NB, NB), NB:] = onehot(hit, -1.0)
        gone = jnp.dot(onehot(hit), jnp.ones((NB, 128), BF), preferred_element_type=F32)
        for j in range(4):
            mask[pl.ds(j, NB, stride=4), :] = gone
        x = xm_ref[pl.ds(b * 1024, 1024), :].astype(F32)
        xm_ref[pl.ds(b * 1024, 1024), :] = jnp.where(mask[...] > 0.5, 0.0, x).astype(BF)

    def lower(k):
        piece = panelf[pl.ds((k % 2) * 8 + k // 2, NB, stride=16), :].astype(BF)
        low = lax.dot_general(
            piece, uinv_ref[...], (((0,), (0,)), ((), ())), preferred_element_type=F32
        )
        m_ref[pl.ds(k * 128, 128), :NB] = low.astype(BF)

    head.step(0)
    fetch.wait()
    for s in range(1, FAR + 3):
        ring.step(s)
        head.step(s)
        if s == 1:
            plane.one()
        if s == 2:
            plane.two()
        if 3 <= s <= 6:
            plane.three(s - 3)
        if s == 7:
            plane.four()
            own_panel.wait()
        if s <= 4:
            swaps(2 * s - 2)
            swaps(2 * s - 1)
        if s == 7:
            panelf[...] = panel[...].astype(F32)
        if s in (8, 9):
            for k in range(8 * (s - 8), 8 * (s - 7)):
                lower(k)
    col = column_of(row)
    rank = ranks(row, col).astype(jnp.int32)
    ids = lax.broadcasted_iota(jnp.int32, (NB, 128), 0)
    lane = lax.broadcasted_iota(jnp.int32, (NB, 128), 1)
    goes = jnp.broadcast_to(col, (NB, 128)) != ids
    slot = jnp.where(
        goes & (rank < CAP), owner_of(jnp.broadcast_to(col, (NB, 128))) * CAP + rank, -1
    )
    stay = jnp.where(goes, -1, ids + NPROW * CAP)
    pieces = [onehot((slot == lane + 128 * u) | (stay == lane + 128 * u)) for u in range(8)]
    chosen = jnp.concatenate(pieces, axis=1)

    own_slot.wait()

    @pl.when(head.root)
    def _():
        head.own(sems.at[3]).wait()

    ring.finish()
    head.finish()
    plane.finish()
    wide[pl.ds(0, NPROW * SLOT), :] = slots[...].astype(F32)
    wide[pl.ds(NPROW * SLOT, 1024), :] = top[...].astype(F32)
    for j in range(4):
        both[:, j * 128 : (j + 1) * 128] = wide[pl.ds(j, 1024, stride=4), :].astype(BF)
    picked = jnp.dot(chosen, both[...], preferred_element_type=F32)
    wide[pl.ds(0, 1024), :] = extra_ref[...].astype(F32)
    more = jnp.concatenate([wide[pl.ds(j, NB, stride=4), :] for j in range(4)], axis=1)
    picked = (picked + more).astype(BF)
    st_ref[pl.ds(0, NB), :] = jnp.dot(
        linv_ref[...], picked, preferred_element_type=F32
    ).astype(BF)
    st_ref[pl.ds(NB, NB), :] = both[pl.ds(NPROW * CAP, NB), :]


def main(tv, picked, pv, linv, uinv, row, extra):
    return pl.pallas_call(
        main_kernel,
        out_shape=(
            jax.ShapeDtypeStruct((8 * NB, 2 * NB), BF),
            jax.ShapeDtypeStruct((8192, 128), BF),
            jax.ShapeDtypeStruct((2 * NB, 2 * NB), BF),
        ),
        in_specs=[spec(ANY)] + [spec(VMEM)] * 6,
        out_specs=(spec(VMEM),) * 3,
        scratch_shapes=[
            VMEM((NPROW * SLOT, 128), BF),
            VMEM((1024, 128), BF),
            VMEM((4096, 128), BF),
            VMEM((4096, 128), F32),
            VMEM((4096, 128), F32),
            VMEM((1024, 512), BF),
            VMEM((1024, 128), F32),
        ]
        + RING_SEMS
        + TOP_SEMS
        + [pltpu.SemaphoreType.DMA((2, 20)), pltpu.SemaphoreType.DMA((2, 20))]
        + [pltpu.SemaphoreType.DMA((4,))],
        compiler_params=pltpu.CompilerParams(
            collective_id=0, has_side_effects=True, vmem_limit_bytes=40 * 2**20
        ),
        name="gather_prepare",
    )(tv, picked, pv, linv, uinv, row, extra)


def update_kernel(m_ref, xm_ref, st_ref, o_ref, spread):
    i = pl.program_id(0)
    product = jnp.dot(
        m_ref[pl.ds(pl.multiple_of(i * NB, NB), NB), :], st_ref[...], preferred_element_type=F32
    )
    for j in range(4):
        spread[pl.ds(j, NB, stride=4), :] = product[:, j * 128 : (j + 1) * 128]
    x = xm_ref[pl.ds(pl.multiple_of(i * 1024, 1024), 1024), :]
    o_ref[...] = (x.astype(F32) - spread[...]).astype(BF)

    @pl.when((i == 0) & (lax.axis_index("prow") == 0))
    def _():
        for j in range(4):
            spread[pl.ds(j, NB, stride=4), :] = st_ref[pl.ds(0, NB), j * 128 : (j + 1) * 128].astype(F32)
        o_ref[...] = spread[...].astype(BF)


def update(m, xm, st):
    return pl.pallas_call(
        update_kernel,
        out_shape=jax.ShapeDtypeStruct((8192, 128), BF),
        grid=(8,),
        in_specs=[spec(VMEM)] * 3,
        out_specs=pl.BlockSpec((1024, 128), lambda i: (i, 0)),
        scratch_shapes=[VMEM((1024, 128), F32)],
        compiler_params=pltpu.CompilerParams(vmem_limit_bytes=16 * 2**20),
        name="update",
    )(m, xm, st)


def per_device(trailing, panel, lower_inverse, upper_inverse, pivots):
    tv = trailing.reshape(8, 256, 2, 2, 128).transpose(0, 1, 3, 2, 4).reshape(8192, 128)
    pv = panel.reshape(16, 8, 2, 128).transpose(0, 2, 1, 3).reshape(256, 128)
    picked, rounds = pick(trailing, pivots, jnp.zeros((1,), jnp.int32))
    extra = later_rounds(trailing, pivots, rounds)
    m, xm, st = main(
        tv, picked, pv, lower_inverse, upper_inverse, pivots.reshape(1, NB), extra
    )
    out = update(m, xm, st)
    return out.reshape(8, 256, 2, 2, 128).transpose(0, 1, 3, 2, 4).reshape(trailing.shape)


def solution(mesh):
    placed = (P(None, "prow", None, "pcol"), P("pcol", None, "prow"), P(), P(), P())
    return jax.shard_map(
        per_device,
        mesh=mesh,
        in_specs=placed,
        out_specs=P(None, "prow", None, "pcol"),
        check_vma=False,
    )
```

time: 261 us -> 53.2 us (0.20)
  waiting for transfers between devices: 213 us -> 0 us
  Pallas kernels: 0 us -> 50.4 us
  local copies, waits for them, and re-layouts: 24.5 us -> 0.33 us
  between operations: 15 us -> 0.08 us
  matrix products: 4.05 us -> 0 us
  other arithmetic: 4.52 us -> 1.7 us
    psum x1 -> x0, waiting for transfers between devices: 213 us -> none  [per_device(): lax.psum(source, 'prow').astype(jnp.float32).astype(jnp.bfloat16)]
    pallas_call x0 -> x3, Pallas kernels: none -> 50.4 us  [the longest x1 41.5 us: main(): pl.pallas_call(main_kernel, out_shape=(jax.ShapeDtypeStruct((8 * NB, 2 *...]
    gather x3 -> x0, local copies, waits for them, and re-layouts: 12.2 us -> none  [the longest x2 11 us: per_device(): jnp.take(root_top, incoming, axis=0)]
    unnamed x16 -> x10, local copies, waits for them, and re-layouts: 7.01 us -> 0.3 us
    reshape x2 -> x0, local copies, waits for them, and re-layouts: 5.35 us -> none  [the longest x1 2.97 us: per_device(): return updated.reshape(trailing.shape)]
    dot_general x2 -> x0, matrix products: 4.05 us -> none  [the longest x1 3.79 us: contract_lead(): lax.dot_general(left_side, right_side, (((0,), (0,)), ((), ())), preferre...]
  transfers between devices with their start and end apart: 2 -> 0, of which waited for: 1 -> 0; matrix products, arithmetic and copies ran while one was open for 6% -> 0% of each run, Pallas kernels for 0% -> 0%
where the time goes in v1:
time: 53.2 us; the launch traced here: 53.1 us
  Pallas kernels  50.4 us (95%)
  other arithmetic  1.7 us (3%)
  loops' own time  0.66 us (1%)
    pallas_call x1, Pallas kernels, main(): pl.pallas_call(main_kernel, out_shape=(jax.ShapeDtypeStruct((8 * NB, 2 *...  41.5 us
    pallas_call x1, Pallas kernels, update(): pl.pallas_call(update_kernel, out_shape=jax.ShapeDtypeStruct((8192, 128),...  4.52 us
    pallas_call x1, Pallas kernels, pick(): pl.pallas_call(pick_kernel, out_shape=(jax.ShapeDtypeStruct((CAP, 2, 256)...  4.37 us

profile of v1, /device:TPU:1, one launch (start us, length us, event | category | flops | bytes accessed | tf_op | source)
XLA Modules:
  0.0 53.1 jit_solution(14254435071197845007)
XLA Ops:
  0.0 0.0 copy-start.5
  0.0 0.0 copy-start.4
  0.0 0.8 %iota_compare_fusion.2 = pred[256]{0:T(512)(128)(4,1)S(1)} fusion(s32[256]{0:T(256)} %piv_ref.1), kind=kLoop, calls=%fused_computation.13 | loop fusion | flops 256 | bytes 1280 | tf_op jit(solution)/shard_map/ne | solution.py:219
  0.8 0.7 %shift-right-arithmetic_and_fusion = s32[256]{0:T(256)S(1)} fusion(s32[256]{0:T(256)} %piv_ref.1), kind=kLoop, calls=%fused_computation.14 | loop fusion | flops 512 | bytes 2048 | tf_op jit(solution)/shard_map/and | solution.py:45
  1.5 0.2 convert_reduce_fusion
  1.7 4.4 %pick_rows.2 = (bf16[24,2,256]{2,1,0:T(2,128)(2,1)S(1)}, s32[1]{0:T(128)}) custom-call(s32[256]{0:T(256)} %piv_ref.1, s32[1]{0:T(128)} %constant.5.clone.1.t_ref, s32[1,256]{1,0:T(1,128)} %bitcast.43, bf16[8,256,2,256]{3,2,1,0:T(2,128)(2,1)} %x_ref.1), custom_call_target="tpu_custom_call" | custom-call | tf_op jit(solution)/shard_map/pick_rows/pallas_call | solution.py:88
  6.1 0.0 copy-done.5
  6.1 0.0 copy-done.4
  6.1 0.0 copy-start.1
  6.2 0.0 copy-start.2
  6.2 0.0 copy-start.3
  6.2 0.7 %while.10 = (s32[]{:T(128)}, bf16[1024,128]{1,0:T(8,128)(2,1)S(1)}, s32[1]{0:T(128)}, s32[256]{0:T(256)S(1)}, pred[256]{0:T(512)(128)(4,1)S(1)}, /*index=5*/s32[...) while((s32[]{:T(128)}, bf16[1024,128]{1,0:T(8,128)(2,1)S(1)}, ...), condition=%wide.region_2.3_spmd, body=%wide.region_1.2_spmd.sunk | while | flops 202180608 | bytes 4034969 | solution.py:234
  6.8 0.2 copy-done.1
  7.1 0.1 copy-done.2
  7.1 0.0 copy-done.3
  7.1 41.5 %gather_prepare.1 = (bf16[2048,512]{1,0:T(8,128)(2,1)S(1)}, bf16[8192,128]{1,0:T(8,128)(2,1)S(1)}, bf16[512,512]{1,0:T(8,128)(2,1)S(1)}) custom-call(bf16[8192,128]{1,0:T(8,128)(2,1)S(1)} %bitcast.42, bf16[96,128]{1,0:T(8,128)(2,1)S(1)} %bitcast.41, bf16[256,128]{1,0:T(8,128)(2,1)S(1)} %bitcast.40, bf16[256,256]{1,0:T(8,128)(2,1)S(1)} %copy-done.1, ...), custom_call_target="tpu_custom_call" | custom-call | tf_op jit(solution)/shard_map/gather_prepare/pallas_call | solution.py:522
  48.6 4.5 %update.1 = bf16[8192,128]{1,0:T(8,128)(2,1)} custom-call(bf16[2048,512]{1,0:T(8,128)(2,1)S(1)} %get-tuple-element.57.m_ref, bf16[8192,128]{1,0:T(8,128)(2,1)S(1)} %get-tuple-element.58.xm_ref, bf16[512,512]{1,0:T(8,128)(2,1)S(1)} %get-tuple-element.59.st_ref), custom_call_target="tpu_custom_call" | custom-call | tf_op jit(solution)/shard_map/update/pallas_call | solution.py:569
  (1 shorter events, 0.0 us)
Async XLA Ops:
  0.0 6.1 %copy-start.5 = (s32[256]{0:T(256)S(1)}, s32[256]{0:T(256)}, u32[]{:S(2)}) copy-start(s32[256]{0:T(256)} %piv_ref.1) | copy-start | bytes 3076
  0.0 6.1 %copy-start.4 = (bf16[8,256,2,256]{3,2,1,0:T(2,128)(2,1)S(1)}, bf16[8,256,2,256]{3,2,1,0:T(2,128)(2,1)}, u32[]{:S(2)}) copy-start(bf16[8,256,2,256]{3,2,1,0:T(2,128)(2,1)} %x_ref.1) | copy-start | bytes 6291460
  6.1 0.9 %copy-start.1 = (bf16[256,256]{1,0:T(8,128)(2,1)S(1)}, bf16[256,256]{1,0:T(8,128)(2,1)}, u32[]{:S(2)}) copy-start(bf16[256,256]{1,0:T(8,128)(2,1)} %linv_ref.1) | copy-start | bytes 393220
  6.2 1.0 %copy-start.2 = (bf16[256,256]{1,0:T(8,128)(2,1)S(1)}, bf16[256,256]{1,0:T(8,128)(2,1)}, u32[]{:S(2)}) copy-start(bf16[256,256]{1,0:T(8,128)(2,1)} %uinv_ref.1) | copy-start | bytes 393220
  6.2 1.0 %copy-start.3 = (bf16[16,8,256]{2,1,0:T(8,128)(2,1)S(1)}, bf16[16,8,256]{2,1,0:T(8,128)(2,1)}, u32[]{:S(2)}) copy-start(bf16[16,8,256]{2,1,0:T(8,128)(2,1)} %param.8) | copy-start | bytes 196612

commit v2 on v1

v2 whole, which is shorter than its diff:
```python
import functools

import jax
import jax.numpy as jnp
from jax import lax
from jax.experimental import pallas as pl
from jax.experimental.pallas import tpu as pltpu
from jax.sharding import PartitionSpec as P

NB = 256
CAP = 20
NZ, NX, NY = 16, 4, 4
NPROW = 2 * NZ
KR = 2
LEVEL = (0, 4, 6, 16)
FAR = NZ // 2
WIDE = NPROW * CAP + NB
SLOT = CAP * 4
TCH = 4
TROWS = 512 // TCH
BF, F32 = jnp.bfloat16, jnp.float32
VMEM, ANY, SMEM = pltpu.VMEM, pl.ANY, pltpu.SMEM


def spec(space):
    return pl.BlockSpec(memory_space=space)


def remote(src, dst, ss, rs, **where):
    return pltpu.make_async_remote_copy(
        src_ref=src, dst_ref=dst, send_sem=ss, recv_sem=rs,
        device_id=where, device_id_type=pl.DeviceIdType.MESH,
    )


def onehot(cond, value=1.0):
    return jnp.where(cond, value, 0.0).astype(BF)


def column_of(row):
    n = row.shape[1]
    eye = lax.broadcasted_iota(jnp.int32, (n, n), 0) == lax.broadcasted_iota(jnp.int32, (n, n), 1)
    return jnp.sum(jnp.where(eye, jnp.broadcast_to(row, (n, n)), 0), axis=1, keepdims=True)


def owner_of(piv):
    return (piv >> 8) & (NPROW - 1)


def ranks(row, col):
    i0 = lax.broadcasted_iota(jnp.int32, (NB, NB), 0)
    i1 = lax.broadcasted_iota(jnp.int32, (NB, NB), 1)
    before = (owner_of(col) == owner_of(row)) & (i1 < i0) & (row != i1)
    return jnp.dot(onehot(before), jnp.ones((NB, 128), BF), preferred_element_type=F32)


def pick_kernel(t_ref, row_ref, x_ref, o_ref, rounds_ref, sem):
    me = lax.axis_index("prow")
    row = row_ref[...]
    col = column_of(row)
    rank = ranks(row, col).astype(jnp.int32)
    ids = lax.broadcasted_iota(jnp.int32, (NB, 128), 0)
    lane = lax.broadcasted_iota(jnp.int32, (NB, 128), 1)
    col = jnp.broadcast_to(col, (NB, 128))
    moved = col != ids
    here = moved & (owner_of(col) == me) & (rank == lane + t_ref[0] * CAP)
    local = ((col >> 13) << 8) + (col & 255)
    index = jnp.sum(jnp.where(here, local, 0), axis=0, keepdims=True)
    copies = []
    for s in range(CAP):
        r = jnp.sum(jnp.where(lane[:1] == s, index, 0))
        copies.append(pltpu.make_async_copy(x_ref.at[r >> 8, r & 255], o_ref.at[s], sem.at[s]))
        copies[-1].start()
    rounds_ref[0] = jnp.max(jnp.where(moved, rank, 0)) // CAP + 1
    for c in copies:
        c.wait()


def pick(trailing, row, t):
    out, rounds = pl.pallas_call(
        pick_kernel,
        out_shape=(
            jax.ShapeDtypeStruct((CAP, 2, 256), BF),
            jax.ShapeDtypeStruct((1,), jnp.int32),
        ),
        in_specs=[spec(SMEM), spec(VMEM), spec(ANY)],
        out_specs=(spec(VMEM), spec(SMEM)),
        scratch_shapes=[pltpu.SemaphoreType.DMA((CAP,))],
        compiler_params=pltpu.CompilerParams(vmem_limit_bytes=16 * 2**20),
        name="pick_rows",
    )(t, row, trailing)
    return out.reshape(CAP, 2, 2, 128).transpose(0, 2, 1, 3).reshape(SLOT, 128), rounds


class Ring:
    def __init__(self, src, slots, zs, zr, ps, pr):
        self.src, self.slots, self.zs, self.zr, self.ps, self.pr = src, slots, zs, zr, ps, pr
        me = lax.axis_index("prow")
        self.z, self.core = me // 2, me % 2

    def rows(self, z, core):
        return self.slots.at[pl.ds(((z % NZ) * 2 + core) * SLOT, SLOT)]

    def to(self, way, hops):
        return ((self.z + NZ + (1 - 2 * way) * hops) % NZ) * 2 + self.core

    def send(self, way, o, hops, src=None):
        dst = self.rows(self.z + NZ - (1 - 2 * way) * (o - hops), self.core)
        c = remote(
            dst if src is None else src, dst, self.zs, self.zr.at[way, o - 1],
            prow=self.to(way, hops),
        )
        c.start()

    def mate(self, offset, src=None):
        dst = self.rows(self.z + NZ + offset, self.core)
        c = remote(
            dst if src is None else src, dst, self.ps, self.pr, prow=self.z * 2 + 1 - self.core
        )
        c.start()

    def begin(self):
        for o in range(KR, 0, -1):
            for way in range(2):
                self.send(way, o, o, self.src)
        self.mate(0, self.src)

    def step(self, o):
        for way in range(2):
            last = FAR - way
            if o > last:
                continue
            dst = self.rows(self.z + NZ - (1 - 2 * way) * o, self.core)
            remote(
                dst, dst, self.zs, self.zr.at[way, o - 1], prow=self.to(0, 0)
            ).wait_recv()
            if o + KR <= last:
                self.send(way, o + KR, KR)
            self.mate(o * (2 * way - 1))

    def finish(self):
        mates = self.slots.at[pl.ds(0, NZ * SLOT)]
        mate = remote(mates, mates, self.ps, self.pr, prow=self.to(0, 0))
        mate.wait_recv()
        mate.wait_send()
        sent = self.slots.at[pl.ds(0, (NZ - 1) * SLOT)]
        remote(sent, sent, self.zs, self.pr, prow=self.to(0, 0)).wait_send()


DMA = pltpu.SemaphoreType.DMA
RING_SEMS = [DMA, DMA((2, FAR)), DMA, DMA]


def greet(ids, meanwhile=None):
    barrier = pltpu.get_barrier_semaphore()
    for where in ids:
        pl.semaphore_signal(barrier, inc=1, device_id=where, device_id_type=pl.DeviceIdType.MESH)
    if meanwhile is not None:
        meanwhile()
    pl.semaphore_wait(barrier, len(ids))


def z_neighbours():
    me = lax.axis_index("prow")
    z, core = me // 2, me % 2
    away = [d for k in range(1, max(KR, 2) + 1) for d in (k, NZ - k)]
    return [{"prow": z * 2 + 1 - core}] + [{"prow": ((z + d) % NZ) * 2 + core} for d in away]


def gather_kernel(src_ref, o_ref, slots, zs, zr, ps, pr, sem):
    greet(z_neighbours())
    ring = Ring(src_ref, slots, zs, zr, ps, pr)
    ring.begin()
    own = pltpu.make_async_copy(src_ref, ring.rows(ring.z, ring.core), sem)
    own.start()
    for s in range(1, FAR + 1):
        ring.step(s)
    own.wait()
    ring.finish()
    o_ref[...] = slots[...]


def gather_round(picked):
    return pl.pallas_call(
        gather_kernel,
        out_shape=jax.ShapeDtypeStruct((NPROW * SLOT, 128), BF),
        in_specs=[spec(VMEM)],
        out_specs=spec(VMEM),
        scratch_shapes=[VMEM((NPROW * SLOT, 128), BF)] + RING_SEMS + [pltpu.SemaphoreType.DMA],
        compiler_params=pltpu.CompilerParams(collective_id=1, has_side_effects=True),
        name="gather_more",
    )(picked)


def later_rounds(trailing, row, rounds):
    def body(carry):
        t, total = carry
        picked, _ = pick(trailing, row, t.reshape(1))
        rows = gather_round(picked).reshape(NPROW * CAP, 512)
        pivots = row[0] + jnp.minimum(t, 0)
        i = jnp.arange(NB, dtype=jnp.int32)
        owner = owner_of(pivots)
        moved = pivots != i
        before = (owner[:, None] == owner[None, :]) & (i[None, :] < i[:, None]) & moved[None, :]
        at = jnp.sum(before.astype(jnp.int32), axis=1) - t * CAP
        slot = jnp.where(moved & (at >= 0) & (at < CAP), owner * CAP + at, -1)
        chosen = onehot(slot[:, None] == jnp.arange(NPROW * CAP, dtype=jnp.int32)[None, :])
        part = jnp.dot(chosen, rows, preferred_element_type=F32).astype(BF)
        return t + 1, total + part.reshape(NB * 4, 128)

    start = (jnp.int32(1), jnp.zeros((NB * 4, 128), BF))
    return lax.while_loop(lambda c: c[0] < rounds[0], body, start)[1]


class Plane:
    OFF = (0, -1, 1, 2)

    def __init__(self, src, out, ss, rs, last):
        self.src, self.out, self.ss, self.rs, self.last = src, out, ss, rs, last
        q = lax.axis_index("pcol")
        self.x, self.y = q // NY, q % NY

    def device(self, h, first, second):
        dx, dy = (second, first) if h == 0 else (first, second)
        return ((self.x + NX + dx) % NX) * NY + (self.y + NY + dy) % NY

    def part(self, h, first, second, quarter=None):
        base = self.device(h, first, second) * 256 + h * 128
        if quarter is None:
            return self.out.at[pl.ds(base, 128)]
        return self.out.at[pl.ds(base + 64 * quarter, 64)]

    def send(self, h, k, to, ref, src=None):
        rs = self.last if k >= 12 else self.rs.at[h, k]
        remote(ref if src is None else src, ref, self.ss, rs, pcol=to).start()

    def wait(self, h, k, ref):
        remote(ref, ref, self.ss, self.rs.at[h, k], pcol=self.device(h, 0, 0)).wait_recv()

    def second(self, h, m, src=None):
        ref = self.part(h, self.OFF[m], 0)
        self.send(h, 4 + m, self.device(h, 0, 1), ref, src)
        self.send(h, 8 + m, self.device(h, 0, -1), ref, src)

    def begin(self):
        for h in range(2):
            own = self.src.at[pl.ds(h * 128, 128)]
            for k, f in enumerate((2, 1, -1)):
                self.send(h, k, self.device(h, f, 0), self.part(h, 0, 0), own)
        for h in range(2):
            self.second(h, 0, self.src.at[pl.ds(h * 128, 128)])

    def one(self):
        for h in range(2):
            self.wait(h, 1, self.part(h, -1, 0))
            self.second(h, 1)
        for h in range(2):
            self.wait(h, 2, self.part(h, 1, 0))
            self.second(h, 2)

    def two(self):
        for h in range(2):
            self.wait(h, 0, self.part(h, -2, 0))
            self.second(h, 3)

    def three(self, m):
        for h in range(2):
            f = self.OFF[m]
            self.wait(h, 4 + m, self.part(h, f, -1))
            self.send(h, 12 + m, self.device(h, 0, 1), self.part(h, f, -1, 0))
            self.wait(h, 8 + m, self.part(h, f, 1))
            self.send(h, 16 + m, self.device(h, 0, -1), self.part(h, f, 1, 1))

    def four(self):
        got = self.out.at[pl.ds(0, 1024)]
        remote(got, got, self.ss, self.last, pcol=self.device(0, 0, 0)).wait_recv()

    def finish(self):
        sent = self.out.at[pl.ds(0, 3840)]
        remote(sent, sent, self.ss, self.last, pcol=self.device(0, 0, 0)).wait_send()


def plane_neighbours():
    q = lax.axis_index("pcol")
    x, y = q // NY, q % NY
    along_x = [{"pcol": ((x + d) % NX) * NY + y} for d in range(1, NX)]
    return along_x + [{"pcol": x * NY + (y + d) % NY} for d in range(1, NY)]


class Top:
    KINDS = ((0, 2), (1, 2), (0, 1), (1, 1))

    def __init__(self, src, out, ss, rr, ps, pr):
        self.src, self.out, self.ss, self.rr, self.ps, self.pr = src, out, ss, rr, ps, pr
        me = lax.axis_index("prow")
        z = me // 2
        self.z, self.core = z, me % 2
        self.root = me == 0
        self.dist = jnp.where(z <= FAR, z, NZ - z)
        self.relay = z % 2 == 0
        self.goes = (
            self.relay & (z <= FAR - 2),
            self.relay & ((z == 0) | (z >= FAR + 4)),
            self.relay & (z >= FAR + 2),
            self.relay & (((z >= 2) & (z <= FAR)) | (z == FAR + 2)),
        )

    def rows(self, ref, half, n):
        return ref.at[pl.ds(half * 512 + n * TROWS, TROWS)]

    def half(self, half):
        return self.out.at[pl.ds(half * 512, 512)]

    def ring(self, k, n, src):
        way, hops = self.KINDS[k]
        to = ((self.z + NZ + (1 - 2 * way) * hops) % NZ) * 2 + self.core
        return remote(
            self.rows(src, self.core, n), self.rows(self.out, self.core, n),
            self.ss.at[k], self.rr.at[n], prow=to,
        )

    def mate(self, half, n, src, rsem):
        return remote(
            self.rows(src, half, n), self.rows(self.out, half, n),
            self.ps.at[half], rsem, prow=self.z * 2 + 1 - self.core,
        )

    def begin(self):
        @pl.when(self.root)
        def _():
            for n in range(TCH):
                self.mate(1, n, self.src, self.rr.at[n]).start()
                self.ring(0, n, self.src).start()
                self.ring(1, n, self.src).start()
            for n in range(TCH):
                self.mate(0, n, self.src, self.pr).start()

    def own(self, sem):
        return pltpu.make_async_copy(self.src.at[pl.ds(0, 1024)], self.out, sem)

    def step(self, who, chunks):
        @pl.when(who & ~self.root)
        def _():
            for n in chunks:
                self.ring(0, n, self.out).wait_recv()
                for k in range(4):
                    @pl.when(self.goes[k])
                    def _():
                        self.ring(k, n, self.out).start()

                @pl.when(self.z != 0)
                def _():
                    self.mate(self.core, n, self.out, self.pr).start()

    def finish(self):
        other, own = self.half(1 - self.core), self.half(self.core)
        me = self.z * 2 + self.core

        @pl.when(~self.root)
        def _():
            remote(other, other, self.ss.at[0], self.pr, prow=me).wait_recv()

        for k in range(4):
            @pl.when(self.goes[k])
            def _():
                remote(own, own, self.ss.at[k], self.pr, prow=me).wait_send()

        @pl.when(self.z != 0)
        def _():
            remote(own, own, self.ps.at[self.core], self.pr, prow=me).wait_send()

        @pl.when(self.root)
        def _():
            for half in range(2):
                ref = self.half(half)
                remote(ref, ref, self.ps.at[half], self.pr, prow=me).wait_send()


TOP_SEMS = [DMA((4,)), DMA((TCH,)), DMA((2,)), DMA]


def main_kernel(
    x_ref, pick_ref, panel_ref, linv_ref, uinv_ref, row_ref, extra_ref,
    m_ref, xm_ref, st_ref,
    slots, top, panel, panelf, wide, both, mask,
    zs, zr, zps, zpr, ts, tr, tps, tpr, ss, rs, last, sems,
):
    me = lax.axis_index("prow")
    ring = Ring(pick_ref, slots, zs, zr, zps, zpr)
    plane = Plane(panel_ref, panel, ss, rs, last)
    head = Top(x_ref, top, ts, tr, tps, tpr)
    row = row_ref[...]
    lanes = lax.broadcasted_iota(jnp.int32, (1, NB), 1)
    moved = row != lanes

    def swaps(b):
        rows = lax.broadcasted_iota(jnp.int32, (NB, NB), 0) + (b * NPROW + me) * NB
        hit = (rows == row) & moved
        m_ref[pl.ds(b * NB, NB), NB:] = onehot(hit, -1.0)
        gone = jnp.dot(onehot(hit), jnp.ones((NB, 128), BF), preferred_element_type=F32)
        for j in range(4):
            mask[pl.ds(j, NB, stride=4), :] = gone
        x = x_ref[pl.ds(b * 1024, 1024), :].astype(F32)
        xm_ref[pl.ds(b * 1024, 1024), :] = jnp.where(mask[...] > 0.5, 0.0, x).astype(BF)

    def lower(k):
        piece = panelf[pl.ds((k % 2) * 8 + k // 2, NB, stride=16), :].astype(BF)
        low = lax.dot_general(
            piece, uinv_ref[...], (((0,), (0,)), ((), ())), preferred_element_type=F32
        )
        m_ref[pl.ds(k * 128, 128), :NB] = low.astype(BF)

    def masks():
        for b in range(8):
            swaps(b)

    greet(z_neighbours() + plane_neighbours(), masks)
    head.begin()
    ring.begin()
    plane.begin()
    q = lax.axis_index("pcol")
    own_panel = pltpu.make_async_copy(panel_ref, panel.at[pl.ds(q * 256, 256)], sems.at[0])
    own_panel.start()
    own_slot = pltpu.make_async_copy(pick_ref, ring.rows(ring.z, ring.core), sems.at[1])
    own_slot.start()

    @pl.when(head.root)
    def _():
        head.own(sems.at[2]).start()

    near, middle, far = [head.relay & ((head.dist >= LEVEL[k]) & (head.dist < LEVEL[k + 1])) for k in range(3)]
    first, second = range(TCH // 2), range(TCH // 2, TCH)
    ring.step(1)
    ring.step(2)
    plane.one()
    plane.two()
    plane.three(0)
    head.step(near, first)
    ring.step(3)
    ring.step(4)
    head.step(near, second)
    head.step(middle, first)
    plane.three(1)
    plane.three(2)
    ring.step(5)
    ring.step(6)
    head.step(middle, second)
    plane.three(3)
    head.step(far, first)
    ring.step(7)
    ring.step(8)
    head.step(far, second)
    plane.four()
    own_panel.wait()
    panelf[...] = panel[...].astype(F32)
    for k in range(16):
        lower(k)
    head.step(~head.relay, range(TCH))
    col = column_of(row)
    rank = ranks(row, col).astype(jnp.int32)
    ids = lax.broadcasted_iota(jnp.int32, (NB, 128), 0)
    lane = lax.broadcasted_iota(jnp.int32, (NB, 128), 1)
    goes = jnp.broadcast_to(col, (NB, 128)) != ids
    slot = jnp.where(
        goes & (rank < CAP), owner_of(jnp.broadcast_to(col, (NB, 128))) * CAP + rank, -1
    )
    stay = jnp.where(goes, -1, ids + NPROW * CAP)
    pieces = [onehot((slot == lane + 128 * u) | (stay == lane + 128 * u)) for u in range(WIDE // 128)]
    chosen = jnp.concatenate(pieces, axis=1)

    own_slot.wait()

    @pl.when(head.root)
    def _():
        head.own(sems.at[2]).wait()

    ring.finish()
    head.finish()
    plane.finish()
    wide[pl.ds(0, NPROW * SLOT), :] = slots[...].astype(F32)
    wide[pl.ds(NPROW * SLOT, 1024), :] = top[...].astype(F32)
    for j in range(4):
        both[:, j * 128 : (j + 1) * 128] = wide[pl.ds(j, WIDE, stride=4), :].astype(BF)
    picked = jnp.dot(chosen, both[...], preferred_element_type=F32)
    wide[pl.ds(0, 1024), :] = extra_ref[...].astype(F32)
    more = jnp.concatenate([wide[pl.ds(j, NB, stride=4), :] for j in range(4)], axis=1)
    picked = (picked + more).astype(BF)
    st_ref[pl.ds(0, NB), :] = jnp.dot(
        linv_ref[...], picked, preferred_element_type=F32
    ).astype(BF)
    st_ref[pl.ds(NB, NB), :] = both[pl.ds(NPROW * CAP, NB), :]


def main(tv, picked, pv, linv, uinv, row, extra):
    return pl.pallas_call(
        main_kernel,
        out_shape=(
            jax.ShapeDtypeStruct((8 * NB, 2 * NB), BF),
            jax.ShapeDtypeStruct((8192, 128), BF),
            jax.ShapeDtypeStruct((2 * NB, 2 * NB), BF),
        ),
        in_specs=[spec(VMEM)] * 7,
        out_specs=(spec(VMEM),) * 3,
        scratch_shapes=[
            VMEM((NPROW * SLOT, 128), BF),
            VMEM((1024, 128), BF),
            VMEM((4096, 128), BF),
            VMEM((4096, 128), F32),
            VMEM((4 * WIDE, 128), F32),
            VMEM((WIDE, 512), BF),
            VMEM((1024, 128), F32),
        ]
        + RING_SEMS
        + TOP_SEMS
        + [DMA, DMA((2, 12)), DMA]
        + [DMA((3,))],
        compiler_params=pltpu.CompilerParams(
            collective_id=0, has_side_effects=True, vmem_limit_bytes=40 * 2**20
        ),
        name="gather_prepare",
    )(tv, picked, pv, linv, uinv, row, extra)


def update_kernel(m_ref, xm_ref, st_ref, o_ref, spread):
    i = pl.program_id(0)
    product = jnp.dot(
        m_ref[pl.ds(pl.multiple_of(i * NB, NB), NB), :], st_ref[...], preferred_element_type=F32
    )
    for j in range(4):
        spread[pl.ds(j, NB, stride=4), :] = product[:, j * 128 : (j + 1) * 128]
    x = xm_ref[pl.ds(pl.multiple_of(i * 1024, 1024), 1024), :]
    o_ref[...] = (x.astype(F32) - spread[...]).astype(BF)

    @pl.when((i == 0) & (lax.axis_index("prow") == 0))
    def _():
        for j in range(4):
            spread[pl.ds(j, NB, stride=4), :] = st_ref[pl.ds(0, NB), j * 128 : (j + 1) * 128].astype(F32)
        o_ref[...] = spread[...].astype(BF)


def update(m, xm, st):
    return pl.pallas_call(
        update_kernel,
        out_shape=jax.ShapeDtypeStruct((8192, 128), BF),
        grid=(8,),
        in_specs=[spec(VMEM)] * 3,
        out_specs=pl.BlockSpec((1024, 128), lambda i: (i, 0)),
        scratch_shapes=[VMEM((1024, 128), F32)],
        compiler_params=pltpu.CompilerParams(vmem_limit_bytes=16 * 2**20),
        name="update",
    )(m, xm, st)


def per_device(trailing, panel, lower_inverse, upper_inverse, pivots):
    tv = trailing.reshape(8, 256, 2, 2, 128).transpose(0, 1, 3, 2, 4).reshape(8192, 128)
    pv = panel.reshape(16, 8, 2, 128).transpose(0, 2, 1, 3).reshape(256, 128)
    row = pivots.reshape(1, NB)
    picked, rounds = pick(trailing, row, jnp.zeros((1,), jnp.int32))
    extra = later_rounds(trailing, row, rounds)
    m, xm, st = main(tv, picked, pv, lower_inverse, upper_inverse, row, extra)
    out = update(m, xm, st)
    return out.reshape(8, 256, 2, 2, 128).transpose(0, 1, 3, 2, 4).reshape(trailing.shape)


def solution(mesh):
    placed = (P(None, "prow", None, "pcol"), P("pcol", None, "prow"), P(), P(), P())
    return jax.shard_map(
        per_device,
        mesh=mesh,
        in_specs=placed,
        out_specs=P(None, "prow", None, "pcol"),
        check_vma=False,
    )
```

time: 53.2 us -> 41.6 us (0.78)
  the two profiles are of different devices: /device:TPU:1 before, /device:TPU:39 now
where the time goes in v2:
time: 41.6 us; the launch traced here: 41.4 us
  Pallas kernels  40.4 us (97%)
  loops' own time  0.68 us (2%)
    pallas_call x1, Pallas kernels, main(): pl.pallas_call(main_kernel, out_shape=(jax.ShapeDtypeStruct((8 * NB, 2 *...  32.7 us
    pallas_call x1, Pallas kernels, update(): pl.pallas_call(update_kernel, out_shape=jax.ShapeDtypeStruct((8192, 128),...  4.52 us
    pallas_call x1, Pallas kernels, pick(): pl.pallas_call(pick_kernel, out_shape=(jax.ShapeDtypeStruct((CAP, 2, 256)...  3.11 us

profile of v2, /device:TPU:39, one launch (start us, length us, event | category | flops | bytes accessed | tf_op | source)
XLA Modules:
  0.0 41.4 jit_solution(11011845636675673044)
XLA Ops:
  0.0 0.0 copy-start.4
  0.0 0.0 copy-start.5
  0.0 3.1 %pick_rows.2 = (bf16[20,2,256]{2,1,0:T(2,128)(2,1)S(1)}, s32[1]{0:T(128)}) custom-call(s32[1]{0:T(128)} %constant.6.clone.1.t_ref, s32[1,256]{1,0:T(1,128)} %bitcast.40, bf16[8,256,2,256]{3,2,1,0:T(2,128)(2,1)} %x_ref.1), custom_call_target="tpu_custom_call" | custom-call | tf_op jit(solution)/shard_map/pick_rows/pallas_call | solution.py:80
  3.2 0.0 copy-done.4
  3.2 0.0 copy-done.5
  3.2 0.0 copy-start.1
  3.2 0.0 copy-start.2
  3.2 0.0 copy-start.3
  3.2 0.7 %while.10 = (s32[]{:T(128)}, bf16[1024,128]{1,0:T(8,128)(2,1)S(1)}, s32[1]{0:T(128)}, s32[256]{0:T(256)S(1)}, s32[1,256]{1,0:T(1,128)S(1)}, /*index=5*/bf16[8,25...) while((s32[]{:T(128)}, bf16[1024,128]{1,0:T(8,128)(2,1)S(1)}, s32[1]{0:T(128)}, s32[256]{0:T(256)S(1)}, ...), condition=%wide.region_2.3_spmd, body=%wide.region_0.2_spmd.sunk | while | flops 168923136 | bytes 3630761 | solution.py:212
  3.9 0.2 copy-done.1
  4.1 0.1 copy-done.2
  4.2 0.0 copy-done.3
  4.2 32.7 %gather_prepare.1 = (bf16[2048,512]{1,0:T(8,128)(2,1)S(1)}, bf16[8192,128]{1,0:T(8,128)(2,1)S(1)}, bf16[512,512]{1,0:T(8,128)(2,1)S(1)}) custom-call(bf16[8192,128]{1,0:T(8,128)(2,1)S(1)} %bitcast.39, bf16[80,128]{1,0:T(8,128)(2,1)S(1)} %bitcast.38, bf16[256,128]{1,0:T(8,128)(2,1)S(1)} %bitcast.37, bf16[256,256]{1,0:T(8,128)(2,1)S(1)} %copy-done.1, ...), custom_call_target="tpu_custom_call" | custom-call | tf_op jit(solution)/shard_map/gather_prepare/pallas_call | solution.py:495
  36.9 4.5 %update.1 = bf16[8192,128]{1,0:T(8,128)(2,1)} custom-call(bf16[2048,512]{1,0:T(8,128)(2,1)S(1)} %get-tuple-element.47.m_ref, bf16[8192,128]{1,0:T(8,128)(2,1)S(1)} %get-tuple-element.48.xm_ref, bf16[512,512]{1,0:T(8,128)(2,1)S(1)} %get-tuple-element.49.st_ref), custom_call_target="tpu_custom_call" | custom-call | tf_op jit(solution)/shard_map/update/pallas_call | solution.py:542
  (1 shorter events, 0.0 us)
Async XLA Ops:
  0.0 3.2 %copy-start.4 = (bf16[8,256,2,256]{3,2,1,0:T(2,128)(2,1)S(1)}, bf16[8,256,2,256]{3,2,1,0:T(2,128)(2,1)}, u32[]{:S(2)}) copy-start(bf16[8,256,2,256]{3,2,1,0:T(2,128)(2,1)} %x_ref.1) | copy-start | bytes 6291460
  0.0 3.2 %copy-start.5 = (s32[256]{0:T(256)S(1)}, s32[256]{0:T(256)}, u32[]{:S(2)}) copy-start(s32[256]{0:T(256)} %param.11) | copy-start | bytes 3076
  3.2 0.9 %copy-start.1 = (bf16[256,256]{1,0:T(8,128)(2,1)S(1)}, bf16[256,256]{1,0:T(8,128)(2,1)}, u32[]{:S(2)}) copy-start(bf16[256,256]{1,0:T(8,128)(2,1)} %linv_ref.1) | copy-start | bytes 393220
  3.2 1.0 %copy-start.2 = (bf16[256,256]{1,0:T(8,128)(2,1)S(1)}, bf16[256,256]{1,0:T(8,128)(2,1)}, u32[]{:S(2)}) copy-start(bf16[256,256]{1,0:T(8,128)(2,1)} %uinv_ref.1) | copy-start | bytes 393220
  3.2 1.0 %copy-start.3 = (bf16[16,8,256]{2,1,0:T(8,128)(2,1)S(1)}, bf16[16,8,256]{2,1,0:T(8,128)(2,1)}, u32[]{:S(2)}) copy-start(bf16[16,8,256]{2,1,0:T(8,128)(2,1)} %param.8) | copy-start | bytes 196612

commit v3 on v2

--- a/solution.py
+++ b/solution.py
@@ -16,6 +16,7 @@
 FAR = NZ // 2
 WIDE = NPROW * CAP + NB
 SLOT = CAP * 4
+STEP = 512
 TCH = 4
 TROWS = 512 // TCH
 BF, F32 = jnp.bfloat16, jnp.float32
@@ -54,7 +55,13 @@
     return jnp.dot(onehot(before), jnp.ones((NB, 128), BF), preferred_element_type=F32)
 
 
-def pick_kernel(t_ref, row_ref, x_ref, o_ref, rounds_ref, sem):
+def pick_kernel(later, *refs):
+    if later:
+        t_ref, row_ref, x_ref, o_ref, most_ref, sem = refs
+        first = t_ref[0] * CAP
+    else:
+        row_ref, x_ref, o_ref, most_ref, sem = refs
+        first = 0
     me = lax.axis_index("prow")
     row = row_ref[...]
     col = column_of(row)
@@ -63,33 +70,35 @@
     lane = lax.broadcasted_iota(jnp.int32, (NB, 128), 1)
     col = jnp.broadcast_to(col, (NB, 128))
     moved = col != ids
-    here = moved & (owner_of(col) == me) & (rank == lane + t_ref[0] * CAP)
+    here = moved & (owner_of(col) == me) & (rank == lane + first)
     local = ((col >> 13) << 8) + (col & 255)
     index = jnp.sum(jnp.where(here, local, 0), axis=0, keepdims=True)
+    at = [jnp.sum(jnp.where(lane[:1] == s, index, 0)) for s in range(CAP)]
+    most_ref[0] = jnp.max(jnp.where(moved, rank, 0))
     copies = []
     for s in range(CAP):
-        r = jnp.sum(jnp.where(lane[:1] == s, index, 0))
-        copies.append(pltpu.make_async_copy(x_ref.at[r >> 8, r & 255], o_ref.at[s], sem.at[s]))
+        src = x_ref.at[(at[s] >> 8) & 7, at[s] & 255]
+        copies.append(pltpu.make_async_copy(src, o_ref.at[s], sem.at[s]))
         copies[-1].start()
-    rounds_ref[0] = jnp.max(jnp.where(moved, rank, 0)) // CAP + 1
     for c in copies:
         c.wait()
 
 
-def pick(trailing, row, t):
-    out, rounds = pl.pallas_call(
-        pick_kernel,
+def pick(trailing, row, t=None):
+    later = t is not None
+    out, most = pl.pallas_call(
+        functools.partial(pick_kernel, later),
         out_shape=(
             jax.ShapeDtypeStruct((CAP, 2, 256), BF),
             jax.ShapeDtypeStruct((1,), jnp.int32),
         ),
-        in_specs=[spec(SMEM), spec(VMEM), spec(ANY)],
+        in_specs=[spec(SMEM)] * later + [spec(VMEM), spec(ANY)],
         out_specs=(spec(VMEM), spec(SMEM)),
         scratch_shapes=[pltpu.SemaphoreType.DMA((CAP,))],
         compiler_params=pltpu.CompilerParams(vmem_limit_bytes=16 * 2**20),
-        name="pick_rows",
-    )(t, row, trailing)
-    return out.reshape(CAP, 2, 2, 128).transpose(0, 2, 1, 3).reshape(SLOT, 128), rounds
+        name="pick_later" if later else "pick_rows",
+    )(*([t] * later), row, trailing)
+    return out.reshape(CAP, 2, 2, 128).transpose(0, 2, 1, 3).reshape(SLOT, 128), most
 
 
 class Ring:
@@ -192,7 +201,7 @@
     )(picked)
 
 
-def later_rounds(trailing, row, rounds):
+def later_rounds(trailing, row, most):
     def body(carry):
         t, total = carry
         picked, _ = pick(trailing, row, t.reshape(1))
@@ -209,7 +218,7 @@
         return t + 1, total + part.reshape(NB * 4, 128)
 
     start = (jnp.int32(1), jnp.zeros((NB * 4, 128), BF))
-    return lax.while_loop(lambda c: c[0] < rounds[0], body, start)[1]
+    return lax.while_loop(lambda c: c[0] * CAP <= most[0], body, start)[1]
 
 
 class Plane:
@@ -382,7 +391,7 @@
 def main_kernel(
     x_ref, pick_ref, panel_ref, linv_ref, uinv_ref, row_ref, extra_ref,
     m_ref, xm_ref, st_ref,
-    slots, top, panel, panelf, wide, both, mask,
+    slots, top, panel, panelf, wide, both, chosen, mask,
     zs, zr, zps, zpr, ts, tr, tps, tpr, ss, rs, last, sems,
 ):
     me = lax.axis_index("prow")
@@ -415,9 +424,9 @@
             swaps(b)
 
     greet(z_neighbours() + plane_neighbours(), masks)
-    head.begin()
     ring.begin()
     plane.begin()
+    head.begin()
     q = lax.axis_index("pcol")
     own_panel = pltpu.make_async_copy(panel_ref, panel.at[pl.ds(q * 256, 256)], sems.at[0])
     own_panel.start()
@@ -427,6 +436,19 @@
     @pl.when(head.root)
     def _():
         head.own(sems.at[2]).start()
+
+    col = column_of(row)
+    rank = ranks(row, col).astype(jnp.int32)
+    ids = lax.broadcasted_iota(jnp.int32, (NB, 128), 0)
+    lane = lax.broadcasted_iota(jnp.int32, (NB, 128), 1)
+    goes = jnp.broadcast_to(col, (NB, 128)) != ids
+    slot = jnp.where(
+        goes & (rank < CAP), owner_of(jnp.broadcast_to(col, (NB, 128))) * CAP + rank, -1
+    )
+    stay = jnp.where(goes, -1, ids + NPROW * CAP)
+    for u in range(WIDE // 128):
+        hit = (slot == lane + 128 * u) | (stay == lane + 128 * u)
+        chosen[:, 128 * u : 128 * (u + 1)] = onehot(hit)
 
     near, middle, far = [head.relay & ((head.dist >= LEVEL[k]) & (head.dist < LEVEL[k + 1])) for k in range(3)]
     first, second = range(TCH // 2), range(TCH // 2, TCH)
@@ -456,18 +478,6 @@
     for k in range(16):
         lower(k)
     head.step(~head.relay, range(TCH))
-    col = column_of(row)
-    rank = ranks(row, col).astype(jnp.int32)
-    ids = lax.broadcasted_iota(jnp.int32, (NB, 128), 0)
-    lane = lax.broadcasted_iota(jnp.int32, (NB, 128), 1)
-    goes = jnp.broadcast_to(col, (NB, 128)) != ids
-    slot = jnp.where(
-        goes & (rank < CAP), owner_of(jnp.broadcast_to(col, (NB, 128))) * CAP + rank, -1
-    )
-    stay = jnp.where(goes, -1, ids + NPROW * CAP)
-    pieces = [onehot((slot == lane + 128 * u) | (stay == lane + 128 * u)) for u in range(WIDE // 128)]
-    chosen = jnp.concatenate(pieces, axis=1)
-
     own_slot.wait()
 
     @pl.when(head.root)
@@ -481,7 +491,7 @@
     wide[pl.ds(NPROW * SLOT, 1024), :] = top[...].astype(F32)
     for j in range(4):
         both[:, j * 128 : (j + 1) * 128] = wide[pl.ds(j, WIDE, stride=4), :].astype(BF)
-    picked = jnp.dot(chosen, both[...], preferred_element_type=F32)
+    picked = jnp.dot(chosen[...], both[...], preferred_element_type=F32)
     wide[pl.ds(0, 1024), :] = extra_ref[...].astype(F32)
     more = jnp.concatenate([wide[pl.ds(j, NB, stride=4), :] for j in range(4)], axis=1)
     picked = (picked + more).astype(BF)
@@ -508,6 +518,7 @@
             VMEM((4096, 128), F32),
             VMEM((4 * WIDE, 128), F32),
             VMEM((WIDE, 512), BF),
+            VMEM((NB, WIDE), BF),
             VMEM((1024, 128), F32),
         ]
         + RING_SEMS
@@ -521,31 +532,37 @@
     )(tv, picked, pv, linv, uinv, row, extra)
 
 
-def update_kernel(m_ref, xm_ref, st_ref, o_ref, spread):
-    i = pl.program_id(0)
-    product = jnp.dot(
-        m_ref[pl.ds(pl.multiple_of(i * NB, NB), NB), :], st_ref[...], preferred_element_type=F32
-    )
-    for j in range(4):
-        spread[pl.ds(j, NB, stride=4), :] = product[:, j * 128 : (j + 1) * 128]
-    x = xm_ref[pl.ds(pl.multiple_of(i * 1024, 1024), 1024), :]
-    o_ref[...] = (x.astype(F32) - spread[...]).astype(BF)
-
-    @pl.when((i == 0) & (lax.axis_index("prow") == 0))
-    def _():
+def update_kernel(m_ref, xm_ref, st_ref, o_ref, spread, out, sem):
+    copies = []
+    for i in range(2048 // STEP):
+        product = jnp.dot(m_ref[pl.ds(i * STEP, STEP), :], st_ref[...], preferred_element_type=F32)
         for j in range(4):
-            spread[pl.ds(j, NB, stride=4), :] = st_ref[pl.ds(0, NB), j * 128 : (j + 1) * 128].astype(F32)
-        o_ref[...] = spread[...].astype(BF)
+            spread[i % 2, pl.ds(j, STEP, stride=4), :] = product[:, j * 128 : (j + 1) * 128]
+        at = pl.ds(i * STEP * 4, STEP * 4)
+        out[at, :] = (xm_ref[at, :].astype(F32) - spread[i % 2]).astype(BF)
+        if i == 0:
+            @pl.when(lax.axis_index("prow") == 0)
+            def _():
+                for j in range(4):
+                    solved = st_ref[pl.ds(0, NB), j * 128 : (j + 1) * 128]
+                    spread[0, pl.ds(j, NB, stride=4), :] = solved.astype(F32)
+                out[pl.ds(0, 4 * NB), :] = spread[0, pl.ds(0, 4 * NB), :].astype(BF)
+
+        copies.append(pltpu.make_async_copy(out.at[at], o_ref.at[at], sem.at[i]))
+        copies[-1].start()
+    for c in copies:
+        c.wait()
 
 
 def update(m, xm, st):
     return pl.pallas_call(
         update_kernel,
         out_shape=jax.ShapeDtypeStruct((8192, 128), BF),
-        grid=(8,),
         in_specs=[spec(VMEM)] * 3,
-        out_specs=pl.BlockSpec((1024, 128), lambda i: (i, 0)),
-        scratch_shapes=[VMEM((1024, 128), F32)],
+        out_specs=spec(ANY),
+        scratch_shapes=[
+            VMEM((2, 4 * STEP, 128), F32), VMEM((8192, 128), BF), DMA((2048 // STEP,))
+        ],
         compiler_params=pltpu.CompilerParams(vmem_limit_bytes=16 * 2**20),
         name="update",
     )(m, xm, st)
@@ -555,8 +572,8 @@
     tv = trailing.reshape(8, 256, 2, 2, 128).transpose(0, 1, 3, 2, 4).reshape(8192, 128)
     pv = panel.reshape(16, 8, 2, 128).transpose(0, 2, 1, 3).reshape(256, 128)
     row = pivots.reshape(1, NB)
-    picked, rounds = pick(trailing, row, jnp.zeros((1,), jnp.int32))
-    extra = later_rounds(trailing, row, rounds)
+    picked, most = pick(trailing, row)
+    extra = later_rounds(trailing, row, most)
     m, xm, st = main(tv, picked, pv, lower_inverse, upper_inverse, row, extra)
     out = update(m, xm, st)
     return out.reshape(8, 256, 2, 2, 128).transpose(0, 1, 3, 2, 4).reshape(trailing.shape)

time: 41.6 us -> 39 us (0.938)
  the two profiles are of different devices: /device:TPU:39 before, /device:TPU:227 now
where the time goes in v3:
time: 39 us; the launch traced here: 38.5 us
  Pallas kernels  37.5 us (96%)
  loops' own time  0.68 us (2%)
    pallas_call x1, Pallas kernels, main(): pl.pallas_call(main_kernel, out_shape=(jax.ShapeDtypeStruct((8 * NB, 2 *...  31.9 us
    pallas_call x1, Pallas kernels, pick(): pl.pallas_call(functools.partial(pick_kernel, later), out_shape=(jax.Shap...  3.09 us
    pallas_call x1, Pallas kernels, update(): pl.pallas_call(update_kernel, out_shape=jax.ShapeDtypeStruct((8192, 128),...  2.49 us

profile of v3, /device:TPU:227, one launch (start us, length us, event | category | flops | bytes accessed | tf_op | source)
XLA Modules:
  0.0 38.5 jit_solution(1535085747045987379)
XLA Ops:
  0.0 0.0 copy-start.4
  0.0 0.0 copy-start.5
  0.0 3.1 %pick_rows.1 = (bf16[20,2,256]{2,1,0:T(2,128)(2,1)S(1)}, s32[1]{0:T(128)}) custom-call(s32[1,256]{1,0:T(1,128)} %bitcast.40, bf16[8,256,2,256]{3,2,1,0:T(2,128)(2,1)} %refs_1_.1), custom_call_target="tpu_custom_call" | custom-call | tf_op jit(solution)/shard_map/pick_rows/pallas_call | solution.py:89
  3.1 0.0 copy-done.4
  3.2 0.0 copy-done.5
  3.2 0.0 copy-start.1
  3.2 0.0 copy-start.2
  3.2 0.0 copy-start.3
  3.2 0.7 %while.10 = (s32[]{:T(128)}, bf16[1024,128]{1,0:T(8,128)(2,1)S(1)}, s32[1]{0:T(128)}, s32[256]{0:T(256)S(1)}, s32[1,256]{1,0:T(1,128)S(1)}, /*index=5*/bf16[8,25...) while((s32[]{:T(128)}, bf16[1024,128]{1,0:T(8,128)(2,1)S(1)}, s32[1]{0:T(128)}, s32[256]{0:T(256)S(1)}, ...), condition=%wide.region_2.3_spmd, body=%wide.region_0.2_spmd.sunk | while | flops 168923136 | bytes 3630773 | solution.py:221
  3.9 0.2 copy-done.1
  4.1 0.1 copy-done.2
  4.1 0.0 copy-done.3
  4.1 31.9 %gather_prepare.1 = (bf16[2048,512]{1,0:T(8,128)(2,1)S(1)}, bf16[8192,128]{1,0:T(8,128)(2,1)S(1)}, bf16[512,512]{1,0:T(8,128)(2,1)S(1)}) custom-call(bf16[8192,128]{1,0:T(8,128)(2,1)S(1)} %bitcast.39, bf16[80,128]{1,0:T(8,128)(2,1)S(1)} %bitcast.38, bf16[256,128]{1,0:T(8,128)(2,1)S(1)} %bitcast.37, bf16[256,256]{1,0:T(8,128)(2,1)S(1)} %copy-done.1, ...), custom_call_target="tpu_custom_call" | custom-call | tf_op jit(solution)/shard_map/gather_prepare/pallas_call | solution.py:505
  36.0 2.5 %update.1 = bf16[8192,128]{1,0:T(8,128)(2,1)} custom-call(bf16[2048,512]{1,0:T(8,128)(2,1)S(1)} %get-tuple-element.47.m_ref, bf16[8192,128]{1,0:T(8,128)(2,1)S(1)} %get-tuple-element.48.xm_ref, bf16[512,512]{1,0:T(8,128)(2,1)S(1)} %get-tuple-element.49.st_ref), custom_call_target="tpu_custom_call" | custom-call | tf_op jit(solution)/shard_map/update/pallas_call | solution.py:558
  (1 shorter events, 0.0 us)
Async XLA Ops:
  0.0 3.1 %copy-start.4 = (bf16[8,256,2,256]{3,2,1,0:T(2,128)(2,1)S(1)}, bf16[8,256,2,256]{3,2,1,0:T(2,128)(2,1)}, u32[]{:S(2)}) copy-start(bf16[8,256,2,256]{3,2,1,0:T(2,128)(2,1)} %refs_1_.1) | copy-start | bytes 6291460
  0.0 3.2 %copy-start.5 = (s32[256]{0:T(256)S(1)}, s32[256]{0:T(256)}, u32[]{:S(2)}) copy-start(s32[256]{0:T(256)} %param.11) | copy-start | bytes 3076
  3.2 0.9 %copy-start.1 = (bf16[256,256]{1,0:T(8,128)(2,1)S(1)}, bf16[256,256]{1,0:T(8,128)(2,1)}, u32[]{:S(2)}) copy-start(bf16[256,256]{1,0:T(8,128)(2,1)} %linv_ref.1) | copy-start | bytes 393220
  3.2 1.0 %copy-start.2 = (bf16[256,256]{1,0:T(8,128)(2,1)S(1)}, bf16[256,256]{1,0:T(8,128)(2,1)}, u32[]{:S(2)}) copy-start(bf16[256,256]{1,0:T(8,128)(2,1)} %uinv_ref.1) | copy-start | bytes 393220
  3.2 1.0 %copy-start.3 = (bf16[16,8,256]{2,1,0:T(8,128)(2,1)S(1)}, bf16[16,8,256]{2,1,0:T(8,128)(2,1)}, u32[]{:S(2)}) copy-start(bf16[16,8,256]{2,1,0:T(8,128)(2,1)} %param.8) | copy-start | bytes 196612

commit v4 on v3

--- a/solution.py
+++ b/solution.py
@@ -12,7 +12,6 @@
 NZ, NX, NY = 16, 4, 4
 NPROW = 2 * NZ
 KR = 2
-LEVEL = (0, 4, 6, 16)
 FAR = NZ // 2
 WIDE = NPROW * CAP + NB
 SLOT = CAP * 4
@@ -143,8 +142,9 @@
             remote(
                 dst, dst, self.zs, self.zr.at[way, o - 1], prow=self.to(0, 0)
             ).wait_recv()
-            if o + KR <= last:
-                self.send(way, o + KR, KR)
+            if o % KR == 0:
+                for hops in range(min(KR, last - o), 0, -1):
+                    self.send(way, o + hops, hops)
             self.mate(o * (2 * way - 1))
 
     def finish(self):
@@ -172,7 +172,7 @@
 def z_neighbours():
     me = lax.axis_index("prow")
     z, core = me // 2, me % 2
-    away = [d for k in range(1, max(KR, 2) + 1) for d in (k, NZ - k)]
+    away = [d for k in sorted({1, 2, 4} | set(range(1, KR + 1))) for d in (k, NZ - k)]
     return [{"prow": z * 2 + 1 - core}] + [{"prow": ((z + d) % NZ) * 2 + core} for d in away]
 
 
@@ -297,7 +297,7 @@
 
 
 class Top:
-    KINDS = ((0, 2), (1, 2), (0, 1), (1, 1))
+    KINDS = (4, -4, 1, -1, 2, -2)
 
     def __init__(self, src, out, ss, rr, ps, pr):
         self.src, self.out, self.ss, self.rr, self.ps, self.pr = src, out, ss, rr, ps, pr
@@ -305,14 +305,17 @@
         z = me // 2
         self.z, self.core = z, me % 2
         self.root = me == 0
-        self.dist = jnp.where(z <= FAR, z, NZ - z)
-        self.relay = z % 2 == 0
         self.goes = (
-            self.relay & (z <= FAR - 2),
-            self.relay & ((z == 0) | (z >= FAR + 4)),
-            self.relay & (z >= FAR + 2),
-            self.relay & (((z >= 2) & (z <= FAR)) | (z == FAR + 2)),
+            (z == 0) | (z == 4),
+            z == 0,
+            (z == 8) | (z == 12) | (z == 14),
+            (z == 2) | (z == 4) | (z == 8) | (z == 12),
+            (z == 8) | (z == 12),
+            (z == 4) | (z == 8),
         )
+        self.near = (z == 0) | (z == 4) | (z == 12)
+        self.middle = (z == 2) | (z == 8) | (z == 14)
+        self.leaf = (z % 4 != 0) & (z != 2) & (z != 14)
 
     def rows(self, ref, half, n):
         return ref.at[pl.ds(half * 512 + n * TROWS, TROWS)]
@@ -321,8 +324,7 @@
         return self.out.at[pl.ds(half * 512, 512)]
 
     def ring(self, k, n, src):
-        way, hops = self.KINDS[k]
-        to = ((self.z + NZ + (1 - 2 * way) * hops) % NZ) * 2 + self.core
+        to = ((self.z + NZ + self.KINDS[k]) % NZ) * 2 + self.core
         return remote(
             self.rows(src, self.core, n), self.rows(self.out, self.core, n),
             self.ss.at[k], self.rr.at[n], prow=to,
@@ -352,7 +354,7 @@
         def _():
             for n in chunks:
                 self.ring(0, n, self.out).wait_recv()
-                for k in range(4):
+                for k in range(6):
                     @pl.when(self.goes[k])
                     def _():
                         self.ring(k, n, self.out).start()
@@ -361,6 +363,12 @@
                 def _():
                     self.mate(self.core, n, self.out, self.pr).start()
 
+    def late(self):
+        @pl.when(self.z == 4)
+        def _():
+            for n in range(TCH):
+                self.ring(2, n, self.out).start()
+
     def finish(self):
         other, own = self.half(1 - self.core), self.half(self.core)
         me = self.z * 2 + self.core
@@ -369,8 +377,8 @@
         def _():
             remote(other, other, self.ss.at[0], self.pr, prow=me).wait_recv()
 
-        for k in range(4):
-            @pl.when(self.goes[k])
+        for k in range(6):
+            @pl.when(self.goes[k] | (self.z == 4) if k == 2 else self.goes[k])
             def _():
                 remote(own, own, self.ss.at[k], self.pr, prow=me).wait_send()
 
@@ -385,7 +393,7 @@
                 remote(ref, ref, self.ps.at[half], self.pr, prow=me).wait_send()
 
 
-TOP_SEMS = [DMA((4,)), DMA((TCH,)), DMA((2,)), DMA]
+TOP_SEMS = [DMA((6,)), DMA((TCH,)), DMA((2,)), DMA]
 
 
 def main_kernel(
@@ -450,34 +458,32 @@
         hit = (slot == lane + 128 * u) | (stay == lane + 128 * u)
         chosen[:, 128 * u : 128 * (u + 1)] = onehot(hit)
 
-    near, middle, far = [head.relay & ((head.dist >= LEVEL[k]) & (head.dist < LEVEL[k + 1])) for k in range(3)]
     first, second = range(TCH // 2), range(TCH // 2, TCH)
     ring.step(1)
     ring.step(2)
     plane.one()
     plane.two()
     plane.three(0)
-    head.step(near, first)
+    head.step(head.near, first)
     ring.step(3)
     ring.step(4)
-    head.step(near, second)
-    head.step(middle, first)
+    head.step(head.near, second)
+    head.late()
     plane.three(1)
     plane.three(2)
+    head.step(head.middle, first)
     ring.step(5)
     ring.step(6)
-    head.step(middle, second)
+    head.step(head.middle, second)
     plane.three(3)
-    head.step(far, first)
     ring.step(7)
     ring.step(8)
-    head.step(far, second)
     plane.four()
     own_panel.wait()
     panelf[...] = panel[...].astype(F32)
     for k in range(16):
         lower(k)
-    head.step(~head.relay, range(TCH))
+    head.step(head.leaf, range(TCH))
     own_slot.wait()
 
     @pl.when(head.root)

time: 39 us -> 40 us (1.026)
  the two profiles are of different devices: /device:TPU:227 before, /device:TPU:1 now
where the time goes in v4:
time: 40 us; the launch traced here: 39.3 us
  Pallas kernels  38.3 us (96%)
  loops' own time  0.68 us (2%)
    pallas_call x1, Pallas kernels, main(): pl.pallas_call(main_kernel, out_shape=(jax.ShapeDtypeStruct((8 * NB, 2 *...  32.7 us
    pallas_call x1, Pallas kernels, pick(): pl.pallas_call(functools.partial(pick_kernel, later), out_shape=(jax.Shap...  3.06 us
    pallas_call x1, Pallas kernels, update(): pl.pallas_call(update_kernel, out_shape=jax.ShapeDtypeStruct((8192, 128),...  2.49 us

profile of v4, /device:TPU:1, one launch (start us, length us, event | category | flops | bytes accessed | tf_op | source)
XLA Modules:
  0.0 39.3 jit_solution(14257727956652255141)
XLA Ops:
  0.0 0.0 copy-start.4
  0.0 0.0 copy-start.5
  0.0 3.1 %pick_rows.1 = (bf16[20,2,256]{2,1,0:T(2,128)(2,1)S(1)}, s32[1]{0:T(128)}) custom-call(s32[1,256]{1,0:T(1,128)} %bitcast.40, bf16[8,256,2,256]{3,2,1,0:T(2,128)(2,1)} %refs_1_.1), custom_call_target="tpu_custom_call" | custom-call | tf_op jit(solution)/shard_map/pick_rows/pallas_call | solution.py:88
  3.1 0.0 copy-done.4
  3.1 0.0 copy-done.5
  3.1 0.0 copy-start.1
  3.1 0.0 copy-start.2
  3.2 0.0 copy-start.3
  3.2 0.7 %while.10 = (s32[]{:T(128)}, bf16[1024,128]{1,0:T(8,128)(2,1)S(1)}, s32[1]{0:T(128)}, s32[256]{0:T(256)S(1)}, s32[1,256]{1,0:T(1,128)S(1)}, /*index=5*/bf16[8,25...) while((s32[]{:T(128)}, bf16[1024,128]{1,0:T(8,128)(2,1)S(1)}, s32[1]{0:T(128)}, s32[256]{0:T(256)S(1)}, ...), condition=%wide.region_2.3_spmd, body=%wide.region_0.2_spmd.sunk | while | flops 168923136 | bytes 3630773 | solution.py:221
  3.9 0.2 copy-done.1
  4.0 0.1 copy-done.2
  4.1 0.0 copy-done.3
  4.1 32.7 %gather_prepare.1 = (bf16[2048,512]{1,0:T(8,128)(2,1)S(1)}, bf16[8192,128]{1,0:T(8,128)(2,1)S(1)}, bf16[512,512]{1,0:T(8,128)(2,1)S(1)}) custom-call(bf16[8192,128]{1,0:T(8,128)(2,1)S(1)} %bitcast.39, bf16[80,128]{1,0:T(8,128)(2,1)S(1)} %bitcast.38, bf16[256,128]{1,0:T(8,128)(2,1)S(1)} %bitcast.37, bf16[256,256]{1,0:T(8,128)(2,1)S(1)} %copy-done.1, ...), custom_call_target="tpu_custom_call" | custom-call | tf_op jit(solution)/shard_map/gather_prepare/pallas_call | solution.py:511
  36.9 2.5 %update.1 = bf16[8192,128]{1,0:T(8,128)(2,1)} custom-call(bf16[2048,512]{1,0:T(8,128)(2,1)S(1)} %get-tuple-element.47.m_ref, bf16[8192,128]{1,0:T(8,128)(2,1)S(1)} %get-tuple-element.48.xm_ref, bf16[512,512]{1,0:T(8,128)(2,1)S(1)} %get-tuple-element.49.st_ref), custom_call_target="tpu_custom_call" | custom-call | tf_op jit(solution)/shard_map/update/pallas_call | solution.py:564
  (1 shorter events, 0.0 us)
Async XLA Ops:
  0.0 3.1 %copy-start.4 = (bf16[8,256,2,256]{3,2,1,0:T(2,128)(2,1)S(1)}, bf16[8,256,2,256]{3,2,1,0:T(2,128)(2,1)}, u32[]{:S(2)}) copy-start(bf16[8,256,2,256]{3,2,1,0:T(2,128)(2,1)} %refs_1_.1) | copy-start | bytes 6291460
  0.0 3.1 %copy-start.5 = (s32[256]{0:T(256)S(1)}, s32[256]{0:T(256)}, u32[]{:S(2)}) copy-start(s32[256]{0:T(256)} %param.11) | copy-start | bytes 3076
  3.1 0.9 %copy-start.1 = (bf16[256,256]{1,0:T(8,128)(2,1)S(1)}, bf16[256,256]{1,0:T(8,128)(2,1)}, u32[]{:S(2)}) copy-start(bf16[256,256]{1,0:T(8,128)(2,1)} %linv_ref.1) | copy-start | bytes 393220
  3.1 1.0 %copy-start.2 = (bf16[256,256]{1,0:T(8,128)(2,1)S(1)}, bf16[256,256]{1,0:T(8,128)(2,1)}, u32[]{:S(2)}) copy-start(bf16[256,256]{1,0:T(8,128)(2,1)} %uinv_ref.1) | copy-start | bytes 393220
  3.2 1.0 %copy-start.3 = (bf16[16,8,256]{2,1,0:T(8,128)(2,1)S(1)}, bf16[16,8,256]{2,1,0:T(8,128)(2,1)}, u32[]{:S(2)}) copy-start(bf16[16,8,256]{2,1,0:T(8,128)(2,1)} %param.8) | copy-start | bytes 196612

commit v5 on v3

--- a/solution.py
+++ b/solution.py
@@ -143,8 +143,9 @@
             remote(
                 dst, dst, self.zs, self.zr.at[way, o - 1], prow=self.to(0, 0)
             ).wait_recv()
-            if o + KR <= last:
-                self.send(way, o + KR, KR)
+            if o % KR == 0:
+                for hops in range(min(KR, last - o), 0, -1):
+                    self.send(way, o + hops, hops)
             self.mate(o * (2 * way - 1))
 
     def finish(self):
@@ -160,12 +161,10 @@
 RING_SEMS = [DMA, DMA((2, FAR)), DMA, DMA]
 
 
-def greet(ids, meanwhile=None):
+def greet(ids):
     barrier = pltpu.get_barrier_semaphore()
     for where in ids:
         pl.semaphore_signal(barrier, inc=1, device_id=where, device_id_type=pl.DeviceIdType.MESH)
-    if meanwhile is not None:
-        meanwhile()
     pl.semaphore_wait(barrier, len(ids))
 
 
@@ -419,11 +418,7 @@
         )
         m_ref[pl.ds(k * 128, 128), :NB] = low.astype(BF)
 
-    def masks():
-        for b in range(8):
-            swaps(b)
-
-    greet(z_neighbours() + plane_neighbours(), masks)
+    greet(z_neighbours() + plane_neighbours())
     ring.begin()
     plane.begin()
     head.begin()
@@ -450,7 +445,12 @@
         hit = (slot == lane + 128 * u) | (stay == lane + 128 * u)
         chosen[:, 128 * u : 128 * (u + 1)] = onehot(hit)
 
-    near, middle, far = [head.relay & ((head.dist >= LEVEL[k]) & (head.dist < LEVEL[k + 1])) for k in range(3)]
+    for b in range(8):
+        swaps(b)
+
+    near, middle, far = [
+        head.relay & ((head.dist >= LEVEL[k]) & (head.dist < LEVEL[k + 1])) for k in range(3)
+    ]
     first, second = range(TCH // 2), range(TCH // 2, TCH)
     ring.step(1)
     ring.step(2)
@@ -468,29 +468,35 @@
     ring.step(6)
     head.step(middle, second)
     plane.three(3)
-    head.step(far, first)
-    ring.step(7)
-    ring.step(8)
-    head.step(far, second)
+    head.step(far, range(TCH))
     plane.four()
     own_panel.wait()
     panelf[...] = panel[...].astype(F32)
     for k in range(16):
         lower(k)
     head.step(~head.relay, range(TCH))
-    own_slot.wait()
+    ring.step(7)
+    ring.step(8)
 
     @pl.when(head.root)
     def _():
         head.own(sems.at[2]).wait()
 
-    ring.finish()
     head.finish()
     plane.finish()
-    wide[pl.ds(0, NPROW * SLOT), :] = slots[...].astype(F32)
     wide[pl.ds(NPROW * SLOT, 1024), :] = top[...].astype(F32)
     for j in range(4):
-        both[:, j * 128 : (j + 1) * 128] = wide[pl.ds(j, WIDE, stride=4), :].astype(BF)
+        both[pl.ds(NPROW * CAP, NB), j * 128 : (j + 1) * 128] = wide[
+            pl.ds(NPROW * SLOT + j, NB, stride=4), :
+        ].astype(BF)
+    st_ref[pl.ds(NB, NB), :] = both[pl.ds(NPROW * CAP, NB), :]
+    own_slot.wait()
+    ring.finish()
+    wide[pl.ds(0, NPROW * SLOT), :] = slots[...].astype(F32)
+    for j in range(4):
+        both[pl.ds(0, NPROW * CAP), j * 128 : (j + 1) * 128] = wide[
+            pl.ds(j, NPROW * CAP, stride=4), :
+        ].astype(BF)
     picked = jnp.dot(chosen[...], both[...], preferred_element_type=F32)
     wide[pl.ds(0, 1024), :] = extra_ref[...].astype(F32)
     more = jnp.concatenate([wide[pl.ds(j, NB, stride=4), :] for j in range(4)], axis=1)
@@ -498,7 +504,6 @@
     st_ref[pl.ds(0, NB), :] = jnp.dot(
         linv_ref[...], picked, preferred_element_type=F32
     ).astype(BF)
-    st_ref[pl.ds(NB, NB), :] = both[pl.ds(NPROW * CAP, NB), :]
 
 
 def main(tv, picked, pv, linv, uinv, row, extra):

time: 39 us -> 39.4 us (1.010)
  the two profiles are of different devices: /device:TPU:227 before, /device:TPU:1 now
where the time goes in v5:
time: 39.4 us; the launch traced here: 39.3 us
  Pallas kernels  38.3 us (97%)
  loops' own time  0.68 us (2%)
    pallas_call x1, Pallas kernels, main(): pl.pallas_call(main_kernel, out_shape=(jax.ShapeDtypeStruct((8 * NB, 2 *...  32.6 us
    pallas_call x1, Pallas kernels, pick(): pl.pallas_call(functools.partial(pick_kernel, later), out_shape=(jax.Shap...  3.19 us
    pallas_call x1, Pallas kernels, update(): pl.pallas_call(update_kernel, out_shape=jax.ShapeDtypeStruct((8192, 128),...  2.5 us

profile of v5, /device:TPU:1, one launch (start us, length us, event | category | flops | bytes accessed | tf_op | source)
XLA Modules:
  0.0 39.3 jit_solution(6414691671059339469)
XLA Ops:
  0.0 0.0 copy-start.4
  0.0 0.0 copy-start.5
  0.0 3.2 %pick_rows.1 = (bf16[20,2,256]{2,1,0:T(2,128)(2,1)S(1)}, s32[1]{0:T(128)}) custom-call(s32[1,256]{1,0:T(1,128)} %bitcast.40, bf16[8,256,2,256]{3,2,1,0:T(2,128)(2,1)} %refs_1_.1), custom_call_target="tpu_custom_call" | custom-call | tf_op jit(solution)/shard_map/pick_rows/pallas_call | solution.py:89
  3.2 0.0 copy-done.4
  3.3 0.0 copy-done.5
  3.3 0.0 copy-start.1
  3.3 0.0 copy-start.2
  3.3 0.0 copy-start.3
  3.3 0.7 %while.10 = (s32[]{:T(128)}, bf16[1024,128]{1,0:T(8,128)(2,1)S(1)}, s32[1]{0:T(128)}, s32[256]{0:T(256)S(1)}, s32[1,256]{1,0:T(1,128)S(1)}, /*index=5*/bf16[8,25...) while((s32[]{:T(128)}, bf16[1024,128]{1,0:T(8,128)(2,1)S(1)}, s32[1]{0:T(128)}, s32[256]{0:T(256)S(1)}, ...), condition=%wide.region_2.3_spmd, body=%wide.region_0.2_spmd.sunk | while | flops 168923136 | bytes 3630773 | solution.py:220
  4.0 0.2 copy-done.1
  4.2 0.1 copy-done.2
  4.2 0.0 copy-done.3
  4.2 32.6 %gather_prepare.1 = (bf16[2048,512]{1,0:T(8,128)(2,1)S(1)}, bf16[8192,128]{1,0:T(8,128)(2,1)S(1)}, bf16[512,512]{1,0:T(8,128)(2,1)S(1)}) custom-call(bf16[8192,128]{1,0:T(8,128)(2,1)S(1)} %bitcast.39, bf16[80,128]{1,0:T(8,128)(2,1)S(1)} %bitcast.38, bf16[256,128]{1,0:T(8,128)(2,1)S(1)} %bitcast.37, bf16[256,256]{1,0:T(8,128)(2,1)S(1)} %copy-done.1, ...), custom_call_target="tpu_custom_call" | custom-call | tf_op jit(solution)/shard_map/gather_prepare/pallas_call | solution.py:510
  36.8 2.5 %update.1 = bf16[8192,128]{1,0:T(8,128)(2,1)} custom-call(bf16[2048,512]{1,0:T(8,128)(2,1)S(1)} %get-tuple-element.47.m_ref, bf16[8192,128]{1,0:T(8,128)(2,1)S(1)} %get-tuple-element.48.xm_ref, bf16[512,512]{1,0:T(8,128)(2,1)S(1)} %get-tuple-element.49.st_ref), custom_call_target="tpu_custom_call" | custom-call | tf_op jit(solution)/shard_map/update/pallas_call | solution.py:563
  (1 shorter events, 0.0 us)
Async XLA Ops:
  0.0 3.2 %copy-start.4 = (bf16[8,256,2,256]{3,2,1,0:T(2,128)(2,1)S(1)}, bf16[8,256,2,256]{3,2,1,0:T(2,128)(2,1)}, u32[]{:S(2)}) copy-start(bf16[8,256,2,256]{3,2,1,0:T(2,128)(2,1)} %refs_1_.1) | copy-start | bytes 6291460
  0.0 3.3 %copy-start.5 = (s32[256]{0:T(256)S(1)}, s32[256]{0:T(256)}, u32[]{:S(2)}) copy-start(s32[256]{0:T(256)} %param.11) | copy-start | bytes 3076
  3.3 0.9 %copy-start.1 = (bf16[256,256]{1,0:T(8,128)(2,1)S(1)}, bf16[256,256]{1,0:T(8,128)(2,1)}, u32[]{:S(2)}) copy-start(bf16[256,256]{1,0:T(8,128)(2,1)} %linv_ref.1) | copy-start | bytes 393220
  3.3 1.0 %copy-start.2 = (bf16[256,256]{1,0:T(8,128)(2,1)S(1)}, bf16[256,256]{1,0:T(8,128)(2,1)}, u32[]{:S(2)}) copy-start(bf16[256,256]{1,0:T(8,128)(2,1)} %uinv_ref.1) | copy-start | bytes 393220
  3.3 1.0 %copy-start.3 = (bf16[16,8,256]{2,1,0:T(8,128)(2,1)S(1)}, bf16[16,8,256]{2,1,0:T(8,128)(2,1)}, u32[]{:S(2)}) copy-start(bf16[16,8,256]{2,1,0:T(8,128)(2,1)} %param.8) | copy-start | bytes 196612

commit v6 on v5

--- a/solution.py
+++ b/solution.py
@@ -11,7 +11,7 @@
 CAP = 20
 NZ, NX, NY = 16, 4, 4
 NPROW = 2 * NZ
-KR = 2
+KR = 3
 LEVEL = (0, 4, 6, 16)
 FAR = NZ // 2
 WIDE = NPROW * CAP + NB
@@ -455,10 +455,10 @@
     ring.step(1)
     ring.step(2)
     plane.one()
+    ring.step(3)
     plane.two()
     plane.three(0)
     head.step(near, first)
-    ring.step(3)
     ring.step(4)
     head.step(near, second)
     head.step(middle, first)

time: 39.4 us -> 40 us (1.015)
  the two profiles are of different devices: /device:TPU:1 before, /device:TPU:241 now
where the time goes in v6:
time: 40 us
  Pallas kernels  38.9 us (97%)
  loops' own time  0.68 us (2%)
    pallas_call x1, Pallas kernels, main(): pl.pallas_call(main_kernel, out_shape=(jax.ShapeDtypeStruct((8 * NB, 2 *...  33.3 us
    pallas_call x1, Pallas kernels, pick(): pl.pallas_call(functools.partial(pick_kernel, later), out_shape=(jax.Shap...  3.12 us
    pallas_call x1, Pallas kernels, update(): pl.pallas_call(update_kernel, out_shape=jax.ShapeDtypeStruct((8192, 128),...  2.5 us

profile of v6, /device:TPU:241, one launch (start us, length us, event | category | flops | bytes accessed | tf_op | source)
XLA Modules:
  0.0 40.0 jit_solution(1419647696433569925)
XLA Ops:
  0.0 0.0 copy-start.4
  0.0 0.0 copy-start.5
  0.0 3.1 %pick_rows.1 = (bf16[20,2,256]{2,1,0:T(2,128)(2,1)S(1)}, s32[1]{0:T(128)}) custom-call(s32[1,256]{1,0:T(1,128)} %bitcast.40, bf16[8,256,2,256]{3,2,1,0:T(2,128)(2,1)} %refs_1_.1), custom_call_target="tpu_custom_call" | custom-call | tf_op jit(solution)/shard_map/pick_rows/pallas_call | solution.py:89
  3.2 0.0 copy-done.4
  3.2 0.0 copy-done.5
  3.2 0.0 copy-start.1
  3.2 0.0 copy-start.2
  3.2 0.0 copy-start.3
  3.2 0.7 %while.10 = (s32[]{:T(128)}, bf16[1024,128]{1,0:T(8,128)(2,1)S(1)}, s32[1]{0:T(128)}, s32[256]{0:T(256)S(1)}, s32[1,256]{1,0:T(1,128)S(1)}, /*index=5*/bf16[8,25...) while((s32[]{:T(128)}, bf16[1024,128]{1,0:T(8,128)(2,1)S(1)}, s32[1]{0:T(128)}, s32[256]{0:T(256)S(1)}, ...), condition=%wide.region_2.3_spmd, body=%wide.region_0.2_spmd.sunk | while | flops 168923136 | bytes 3630773 | solution.py:220
  3.9 0.2 copy-done.1
  4.1 0.1 copy-done.2
  4.2 0.0 copy-done.3
  4.2 33.3 %gather_prepare.1 = (bf16[2048,512]{1,0:T(8,128)(2,1)S(1)}, bf16[8192,128]{1,0:T(8,128)(2,1)S(1)}, bf16[512,512]{1,0:T(8,128)(2,1)S(1)}) custom-call(bf16[8192,128]{1,0:T(8,128)(2,1)S(1)} %bitcast.39, bf16[80,128]{1,0:T(8,128)(2,1)S(1)} %bitcast.38, bf16[256,128]{1,0:T(8,128)(2,1)S(1)} %bitcast.37, bf16[256,256]{1,0:T(8,128)(2,1)S(1)} %copy-done.1, ...), custom_call_target="tpu_custom_call" | custom-call | tf_op jit(solution)/shard_map/gather_prepare/pallas_call | solution.py:510
  37.5 2.5 %update.1 = bf16[8192,128]{1,0:T(8,128)(2,1)} custom-call(bf16[2048,512]{1,0:T(8,128)(2,1)S(1)} %get-tuple-element.47.m_ref, bf16[8192,128]{1,0:T(8,128)(2,1)S(1)} %get-tuple-element.48.xm_ref, bf16[512,512]{1,0:T(8,128)(2,1)S(1)} %get-tuple-element.49.st_ref), custom_call_target="tpu_custom_call" | custom-call | tf_op jit(solution)/shard_map/update/pallas_call | solution.py:563
  (1 shorter events, 0.0 us)
Async XLA Ops:
  0.0 3.2 %copy-start.4 = (bf16[8,256,2,256]{3,2,1,0:T(2,128)(2,1)S(1)}, bf16[8,256,2,256]{3,2,1,0:T(2,128)(2,1)}, u32[]{:S(2)}) copy-start(bf16[8,256,2,256]{3,2,1,0:T(2,128)(2,1)} %refs_1_.1) | copy-start | bytes 6291460
  0.0 3.2 %copy-start.5 = (s32[256]{0:T(256)S(1)}, s32[256]{0:T(256)}, u32[]{:S(2)}) copy-start(s32[256]{0:T(256)} %param.11) | copy-start | bytes 3076
  3.2 0.9 %copy-start.1 = (bf16[256,256]{1,0:T(8,128)(2,1)S(1)}, bf16[256,256]{1,0:T(8,128)(2,1)}, u32[]{:S(2)}) copy-start(bf16[256,256]{1,0:T(8,128)(2,1)} %linv_ref.1) | copy-start | bytes 393220
  3.2 1.0 %copy-start.2 = (bf16[256,256]{1,0:T(8,128)(2,1)S(1)}, bf16[256,256]{1,0:T(8,128)(2,1)}, u32[]{:S(2)}) copy-start(bf16[256,256]{1,0:T(8,128)(2,1)} %uinv_ref.1) | copy-start | bytes 393220
  3.2 1.0 %copy-start.3 = (bf16[16,8,256]{2,1,0:T(8,128)(2,1)S(1)}, bf16[16,8,256]{2,1,0:T(8,128)(2,1)}, u32[]{:S(2)}) copy-start(bf16[16,8,256]{2,1,0:T(8,128)(2,1)} %param.8) | copy-start | bytes 196612
